TPU v7x, 256 devices: a whole 4x4x8 slice. The times are simulated.
256 devices in a mesh: blk: 64 (over x, z, y_lo), uly: 4 (over y_hi, core).
Axes of the slice: x: 4, y: 4 (y_hi: 2, y_lo: 2; y = y_hi * 2 + y_lo), z: 8, core: 2. Of those that a mesh axis runs over, the one named last changes fastest.
Arguments:
- tokens: bfloat16 [6144, 2560], P(('blk', 'uly')), may hold values from -6 to 6
- in_bits: int32 [6144, 2560], P(('blk', 'uly')), may hold values from 0 to 1
- qkv_weights: bfloat16 [2, 3, 2560, 2560], P(None, None, 'blk', 'uly'), may hold values from -0.125 to 0.125
- qkv_bits: int32 [6144, 3, 2560], P('blk', None, 'uly'), may hold values from 0 to 1
- gain_query: float32 [2560], P('uly'), may hold values from 0.7 to 1.8
- gain_key: float32 [2560], P('uly'), may hold values from 0.7 to 1.8
- out_weights: bfloat16 [2, 2560, 2560], P(None, 'uly', 'blk'), may hold values from -0.5 to 0.5
- mix_bits: int32 [6144, 2560], P('blk', 'uly'), may hold values from 0 to 1
- out_bits: int32 [6144, 2560], P('blk'), may hold values from 0 to 1
Outputs:
- layer_output: bfloat16 [6144, 2560], P(('blk', 'uly'))
Inputs may be any that keep to these rules, and one draw needn't show every extreme that they name: `in_bits`: a bit of 1 stands for the sign +1, a bit of 0 for -1. `qkv_bits`: a bit of 1 stands for the sign +1, a bit of 0 for -1. `mix_bits`: a bit of 1 stands for the sign +1, a bit of 0 for -1. `out_bits`: a bit of 1 stands for the sign +1, a bit of 0 for -1.
All inputs are finite; a program needn't handle non-finite values.
Results may differ from a plain program's by a relative error of at most 0.018.
Values may be sent and summed in bfloat16 or wider, within the bound.
A program may use at most 128 MiB of HBM per device.

v0:
```python
import math

import jax
import jax.numpy as jnp
from jax import lax
from jax.sharding import PartitionSpec as P

HEAD = 128


epsilon = 1e-06


def signed(bit_values):
    return (2 * bit_values - 1).astype(jnp.float32)


def normalize(values, gain_vector):
    row_count = values.shape[0]
    by_head = values.astype(jnp.float32).reshape(row_count, -1, HEAD)
    inverse_rms = lax.rsqrt(jnp.mean(by_head * by_head, axis=-1, keepdims=True) + epsilon)
    return (by_head * inverse_rms * gain_vector.reshape(-1, HEAD)).astype(jnp.bfloat16)


def body(
    tokens, in_bits, qkv_weights, qkv_bits, gain_query, gain_key, out_weights, mix_bits, out_bits
):
    flipped = (tokens.astype(jnp.float32) * signed(in_bits)).astype(jnp.bfloat16)
    group_rows = lax.all_gather(jnp.stack([tokens, flipped]), "uly", axis=1, tiled=True)
    row_total = group_rows.shape[1]
    projections = jnp.einsum(
        "mrd,mkdc->rmkc",
        group_rows,
        lax.all_gather(qkv_weights, "blk", axis=2, tiled=True),
        preferred_element_type=jnp.float32,
    )
    projected = (projections[:, 0] + signed(qkv_bits) * projections[:, 1]).astype(jnp.bfloat16)
    queries = normalize(projected[:, 0], gain_query)
    head_count = queries.shape[1]
    keys_normed = normalize(projected[:, 1], gain_key).reshape(row_total, -1)
    values_block = projected[:, 2]
    score_scale = 1.0 / math.sqrt(HEAD)

    def attend(running, shard_piece):
        numerator, denominator = running
        key_rows = shard_piece[0].reshape(shard_piece[0].shape[0], head_count, HEAD)
        value_rows = shard_piece[1].reshape(shard_piece[1].shape[0], head_count, HEAD)
        scores = (
            jnp.einsum("rhd,nhd->hrn", queries, key_rows, preferred_element_type=jnp.float32)
            * score_scale
        )
        weights = jnp.exp(scores).astype(jnp.bfloat16)
        numerator = numerator + jnp.einsum(
            "hrn,nhd->rhd", weights, value_rows, preferred_element_type=jnp.float32
        )
        denominator = denominator + jnp.sum(weights.astype(jnp.float32), axis=2).T
        return (numerator, denominator)

    start_state = (
        jnp.zeros((row_total, head_count, HEAD), jnp.float32),
        jnp.zeros((row_total, head_count), jnp.float32),
    )
    all_keys, all_values = (
        lax.all_gather(keys_normed, "blk", axis=0, tiled=True),
        lax.all_gather(values_block, "blk", axis=0, tiled=True),
    )
    group_count = lax.axis_size("blk")
    per_block = 1
    while per_block * row_total < 512 and group_count % (per_block * 2) == 0:
        per_block = per_block * 2
    block_rows = per_block * row_total
    block_count = group_count // per_block
    key_blocks = all_keys.reshape(block_count, block_rows, all_keys.shape[1])
    value_blocks = all_values.reshape(block_count, block_rows, all_values.shape[1])

    def scan_step(running, block_pair):
        return (attend(running, block_pair), None)

    (numerator, denominator), unused = lax.scan(scan_step, start_state, (key_blocks, value_blocks))
    attended = (numerator / denominator[:, :, None]).astype(jnp.bfloat16).reshape(row_total, -1)
    attended_flipped = (attended.astype(jnp.float32) * signed(mix_bits)).astype(jnp.bfloat16)
    attended_pair = jnp.stack([attended, attended_flipped])
    out_signs = signed(out_bits)
    partial_out = jnp.einsum(
        "mrc,mcn->rmn",
        attended_pair,
        lax.all_gather(out_weights, "blk", axis=2, tiled=True),
        preferred_element_type=jnp.float32,
    )
    summed = lax.psum_scatter(
        partial_out.astype(jnp.bfloat16), "uly", scatter_dimension=0, tiled=True
    ).astype(jnp.float32)
    own_rows = summed.shape[0]
    own_signs = lax.dynamic_slice_in_dim(out_signs, lax.axis_index("uly") * own_rows, own_rows, 0)
    result_rows = summed[:, 0] + own_signs * summed[:, 1]
    return result_rows.astype(jnp.bfloat16)


def solution(mesh):
    return jax.shard_map(
        body,
        mesh=mesh,
        in_specs=(
            P(("blk", "uly"), None),
            P(("blk", "uly"), None),
            P(None, None, "blk", "uly"),
            P("blk", None, "uly"),
            P("uly"),
            P("uly"),
            P(None, "uly", "blk"),
            P("blk", "uly"),
            P("blk", None),
        ),
        out_specs=P(("blk", "uly"), None),
        check_vma=False,
    )
```

profile of v0, /device:TPU:1, one launch (start us, length us, event | category | flops | bytes accessed | tf_op | source)
XLA Modules:
  0.0 1435.4 jit_solution(2879353111804736999)
XLA Ops:
  6.5 0.7 all-gather.6.cloned.1.call-update
  7.3 1.1 fusion.17
  8.4 0.9 pad_maximum_fusion
  9.3 12.7 all_gather.15
  22.0 423.9 %all-gather.6.cloned.1.call-done = bf16[2,3,2560,640]{3,2,1,0:T(8,128)(2,1)} async-done(((bf16[2,3,40,640]{3,2,1,0:T(8,128)(2,1)}), bf16[2,3,2560,640]{3,2,1,0:T(8,128)(2,1)}) %all-gather.6.cloned.1.call-update) | async-done | bytes 19660816 | tf_op jit(solution)/shard_map/all_gather | solution.py:34
  445.9 8.3 convolution_bitcast_fusion.1
  454.2 0.2 fusion.5
  454.4 0.2 copy.28
  454.8 0.7 fusion.8
  455.6 0.7 slice_convert_fusion
  456.4 0.5 all-gather.10.cloned.1.call-update
  457.0 0.2 copy.30
  457.5 268.4 %all-gather.8.cloned.1.call-done = bf16[6144,640]{1,0:T(8,128)(2,1)} async-done(((bf16[96,640]{1,0:T(8,128)(2,1)}), bf16[6144,640]{1,0:T(8,128)(2,1)}) %all-gather.8.cloned.1.call-update) | async-done | bytes 7864336 | tf_op jit(solution)/shard_map/all_gather | solution.py:64
  726.0 311.0 %all-gather.12.cloned.1.call-done = bf16[6144,1,640]{2,0,1:T(8,128)(2,1)} async-done(((bf16[96,1,640]{2,0,1:T(8,128)(2,1)}), bf16[6144,1,640]{2,0,1:T(8,128)(2,1)}) %all-gather.12.cloned.1.call-update) | async-done | bytes 7864336 | tf_op jit(solution)/shard_map/all_gather | solution.py:65
  1037.0 31.7 %while.13 = (s32[]{:T(128)}, f32[96,5,128]{2,0,1:T(8,128)S(1)}, f32[96,5]{0,1:T(8,128)S(1)}, bf16[8,768,640]{2,1,0:T(8,128)(2,1)}, bf16[8,768,640]{2,1,0:T(8,128...) while((s32[]{:T(128)}, f32[96,5,128]{2,0,1:T(8,128)S(1)}, ...), condition=%wide.region_4.5_spmd.clone, body=%wide.region_2.4_spmd.clone.sunk | while | flops 190341600 | bytes 11927140 | solution.py:79
  1037.0 1.7 constant_dynamic-slice_fusion.3
  1038.7 0.6 copy.51
  1039.3 0.5 convert_reduce_fusion.2
  1039.8 0.6 copy.50
  1040.5 0.5 fusion.35
  1040.9 1.7 constant_dynamic-slice_fusion.3
  1042.6 0.6 copy.51
  1043.3 0.5 convert_reduce_fusion.2
  1043.8 0.6 copy.50
  1044.4 0.5 fusion.35
  1044.9 1.7 constant_dynamic-slice_fusion.3
  1046.6 0.6 copy.51
  1047.3 0.5 convert_reduce_fusion.2
  1047.7 0.6 copy.50
  1048.4 0.5 fusion.35
  1048.9 1.7 constant_dynamic-slice_fusion.3
  1050.6 0.6 copy.51
  1051.2 0.5 convert_reduce_fusion.2
  1051.7 0.6 copy.50
  1052.4 0.5 fusion.35
  1052.9 1.7 constant_dynamic-slice_fusion.3
  1054.5 0.6 copy.51
  1055.2 0.5 convert_reduce_fusion.2
  1055.7 0.6 copy.50
  1056.3 0.5 fusion.35
  1056.8 1.7 constant_dynamic-slice_fusion.3
  1058.5 0.6 copy.51
  1059.2 0.5 convert_reduce_fusion.2
  1059.6 0.6 copy.50
  1060.3 0.5 fusion.35
  1060.8 1.7 constant_dynamic-slice_fusion.3
  1062.5 0.6 copy.51
  1063.1 0.5 convert_reduce_fusion.2
  1063.6 0.6 copy.50
  1064.3 0.5 fusion.35
  1064.8 1.7 constant_dynamic-slice_fusion.3
  1066.4 0.6 copy.51
  1067.1 0.5 convert_reduce_fusion.2
  1067.6 0.6 copy.50
  1068.2 0.5 fusion.35
  1069.0 0.2 copy.34
  1069.2 0.2 copy.36
  1069.5 1.0 fusion.18
  1070.5 274.9 %all-gather.10.cloned.1.call-done = bf16[2,640,2560]{1,2,0:T(8,128)(2,1)} async-done(((bf16[2,640,40]{1,2,0:T(8,128)(2,1)}), bf16[2,640,2560]{1,2,0:T(8,128)(2,1)}) %all-gather.10.cloned.1.call-update) | async-done | bytes 6553616 | tf_op jit(solution)/shard_map/all_gather | solution.py:87
  1345.4 5.0 fusion.1
  1350.3 1.0 copy.46
  1351.4 74.8 %reduce-scatter.4.cloned.1.call-done = bf16[24,5120]{1,0:T(8,128)(2,1)} async-done(((bf16[96,5120]{1,0:T(8,128)(2,1)}), bf16[24,5120]{1,0:T(8,128)(2,1)}) %reduce-scatter.4.cloned.1.call-update) | async-done | bytes 245776
  1426.2 1.0 bitcast_convert_fusion
  1427.2 1.7 fusion.11
  (36 shorter events, 1.3 us)
Async XLA Ops:
  6.5 439.4 %all-gather.6.cloned.1.call-start = ((), (), s32[]{:S(2)}) async-start(), calls=%async_computation.1 | async-start | bytes 19968000 | tf_op jit(solution)/shard_map/all_gather | solution.py:34
  7.3 718.7 %all-gather.8.cloned.1.call-start = ((), (), s32[]{:S(2)}) async-start(), calls=%async_computation.2 | async-start | bytes 7987200 | tf_op jit(solution)/shard_map/all_gather | solution.py:64
  22.0 432.2 %copy-start = (s32[96,3,640]{2,0,1:T(8,128)S(1)}, s32[96,3,640]{2,0,1:T(8,128)}, u32[]{:S(2)}) copy-start(s32[96,3,640]{2,0,1:T(8,128)} %param.14) | copy-start | bytes 2211844
  22.0 432.8 %copy-start.1 = (f32[640]{0:T(1024)S(1)}, f32[640]{0:T(1024)}, u32[]{:S(2)}) copy-start(f32[640]{0:T(1024)} %param.16) | copy-start | bytes 7684
  454.2 3.0 copy-start.2
  455.6 581.4 %all-gather.12.cloned.1.call-start = ((), (), s32[]{:S(2)}) async-start(), calls=%async_computation.4 | async-start | bytes 7987200 | tf_op jit(solution)/shard_map/all_gather | solution.py:65
  456.3 889.0 %all-gather.10.cloned.1.call-start = ((), (), s32[]{:S(2)}) async-start(), calls=%async_computation.3 | async-start | bytes 6656000 | tf_op jit(solution)/shard_map/all_gather | solution.py:87
  456.9 969.3 %reduce-scatter.4.cloned.1.call-start = ((), (), s32[]{:S(2)}) async-start(), calls=%async_computation.5 | async-start | bytes 1228800
Sparse Core Ops, SparseCore 0:
  9.2 436.6 all-gather.5
  455.7 270.2 all-gather.7
  727.7 309.1 all-gather.11
  1038.6 306.6 all-gather.9
  1351.5 74.6 reduce-scatter.3
where the time goes:
time: 1440 us
  waiting for transfers between devices  1350 us (94%)
  local copies, waits for them, and re-layouts  26.1 us (2%)
  matrix products  20.8 us (1%)
    all_gather x1, waiting for transfers between devices, body(): lax.all_gather(qkv_weights, 'blk', axis=2, tiled=True)  424 us
    all_gather x1, waiting for transfers between devices, body(): lax.all_gather(values_block, 'blk', axis=0, tiled=True)  311 us
    all_gather x1, waiting for transfers between devices, body(): lax.all_gather(out_weights, 'blk', axis=2, tiled=True)  275 us
    all_gather x1, waiting for transfers between devices, body(): lax.all_gather(keys_normed, 'blk', axis=0, tiled=True)  268 us
    unnamed x6, waiting for transfers between devices  76.1 us
  transfers between devices with their start and end apart: 5, of which 5 were waited for; matrix products, arithmetic and copies ran while one was open for 3% of the time, Pallas kernels for 0%

commit v1 on v0

v1 whole, which is shorter than its diff:
```python
import functools
import math

import jax
import jax.numpy as jnp
from jax import lax
from jax.experimental import pallas as pl
from jax.experimental.pallas import tpu as pltpu
from jax.sharding import PartitionSpec as P

HEAD = 128
NX, NY, NZ, NC = 4, 4, 8, 2
GROUP = 8
EPSILON = 1e-06
MESH = pl.DeviceIdType.MESH
BF16 = jnp.bfloat16
F32 = jnp.float32


def signed(bits):
    return (2 * bits - 1).astype(F32)


def place():
    blk, uly = lax.axis_index("blk"), lax.axis_index("uly")
    return blk // 16, (uly // 2) * 2 + blk % 2, (blk // 2) % 8, uly % 2


def device(x, y, z, c):
    return {"blk": x * 16 + z * 2 + y % 2, "uly": (y // 2) * 2 + c}


def row_slot(x, y, c):
    return x * 8 + (y % 2) * 4 + (y // 2) * 2 + c


class Mover:
    def __init__(self, send, recv, me):
        self.send, self.recv, self.me, self.sent = send, recv, me, []

    def put(self, src, dst, slot, where):
        copy = pltpu.make_async_remote_copy(
            src_ref=src,
            dst_ref=dst,
            send_sem=self.send.at[len(self.sent)],
            recv_sem=self.recv.at[slot],
            device_id=where,
            device_id_type=MESH,
        )
        copy.start()
        self.sent.append(copy)

    def got(self, ref, slot):
        pltpu.make_async_remote_copy(
            src_ref=ref,
            dst_ref=ref,
            send_sem=self.send.at[0],
            recv_sem=self.recv.at[slot],
            device_id=self.me,
            device_id_type=MESH,
        ).wait_recv()

    def finish(self):
        for copy in self.sent:
            copy.wait_send()


def greet(partners):
    barrier = pltpu.get_barrier_semaphore()
    for partner in partners:
        pl.semaphore_signal(barrier, inc=1, device_id=partner, device_id_type=MESH)
    pl.semaphore_wait(barrier, len(partners))


def group_peer(x, y, z, c, d):
    there = (x * 2 + y % 2 + d) % GROUP
    return device(there // 2, (y // 2) * 2 + there % 2, z, c), there


def comm(kernel, args, outs, sends, recvs, locals_, collective_id):
    return pl.pallas_call(
        kernel,
        out_shape=outs,
        in_specs=[pl.BlockSpec(memory_space=pl.ANY)] * len(args),
        out_specs=[pl.BlockSpec(memory_space=pl.ANY)] * len(outs),
        scratch_shapes=[
            pltpu.SemaphoreType.DMA((sends,)),
            pltpu.SemaphoreType.DMA((recvs,)),
            pltpu.SemaphoreType.DMA((locals_,)),
        ],
        compiler_params=pltpu.CompilerParams(collective_id=collective_id, has_side_effects=True),
    )(*args)


def gather_kernel(xs, wj, wo, sg, xg, wg, wog, sgg, send, recv, loc):
    x, y, z, c = place()
    low = y % 2
    me = device(x, y, z, c)
    own_group = x * 2 + low
    a = x * (1 - c) + y * c
    b = y * (1 - c) + x * c

    def at(first, second):
        return first * (1 - c) + second * c, second * (1 - c) + first * c

    def dev_at(first, second):
        px, py = at(first % 4, second % 4)
        return device(px, py, z, c)

    def slot_at(first, second):
        px, py = at(first % 4, second % 4)
        return row_slot(px, py, c)

    a_up, a_down = dev_at(a + 1, b), dev_at(a + 3, b)
    b_up, b_down = dev_at(a, b + 1), dev_at(a, b + 3)
    z_up, z_down = device(x, y, (z + 1) % NZ, c), device(x, y, (z + 7) % NZ, c)
    twin = device(x, y, z, 1 - c)
    peers = [group_peer(x, y, z, c, d) for d in range(1, GROUP)]
    other_y = device(x, (y + 3 + 2 * (y % 2)) % 4, z, c)
    greet([peer for peer, _ in peers] + [other_y, twin, z_up, z_down])

    mover = Mover(send, recv, me)
    own = slot_at(a, b)
    local = [
        pltpu.make_async_copy(wj.at[own_group], wg.at[:, x, z, low], loc.at[0]),
        pltpu.make_async_copy(xs, xg.at[:, own], loc.at[1]),
        pltpu.make_async_copy(wo, wog.at[:, z], loc.at[2]),
        pltpu.make_async_copy(sg.at[own_group], sgg.at[own_group], loc.at[3]),
    ]
    for copy in local:
        copy.start()

    def w_slot(d):
        return d - 1

    def s_slot(d):
        return 7 + d - 1

    A1, A2, B1U, B1D, B2U, B2D, TWIN, ZW, ZO = 14, 16, 18, 22, 26, 30, 34, 50, 58

    for d, (peer, there) in enumerate(peers, 1):
        mover.put(wj.at[there], wg.at[:, x, z, low], w_slot(d), peer)
    mover.put(xs, xg.at[:, own], A1, a_up)
    mover.put(xs, xg.at[:, own], A1 + 1, a_down)
    mover.put(xs, xg.at[:, own], B1U, b_up)
    mover.put(xs, xg.at[:, own], B1D, b_down)
    mover.put(xs, xg.at[:, own], TWIN, twin)
    for d, (peer, there) in enumerate(peers, 1):
        mover.put(sg.at[there], sgg.at[own_group], s_slot(d), peer)

    local[0].wait()
    for d in range(1, GROUP):
        mover.got(wg.at[:, x, z, low], w_slot(d))

    def z_step(t, source_down, source_up):
        if t < 4:
            mover.put(wg.at[:, :, source_down], wg.at[:, :, source_down], ZW + 2 * (t - 1), z_up)
            mover.put(wg.at[:, :, source_up], wg.at[:, :, source_up], ZW + 2 * (t - 1) + 1, z_down)
        else:
            mover.put(wg.at[0, :, source_down], wg.at[0, :, source_down], ZW + 6, z_up)
            mover.put(wg.at[1, :, source_up], wg.at[1, :, source_up], ZW + 7, z_down)

    def o_step(t, source_down, source_up):
        if t < 4:
            mover.put(wog.at[:, source_down], wog.at[:, source_down], ZO + 2 * (t - 1), z_up)
            mover.put(wog.at[:, source_up], wog.at[:, source_up], ZO + 2 * (t - 1) + 1, z_down)
        else:
            mover.put(wog.at[0, source_down], wog.at[0, source_down], ZO + 6, z_up)
            mover.put(wog.at[1, source_up], wog.at[1, source_up], ZO + 7, z_down)

    def z_got(t):
        down, up = (z + 8 - t) % NZ, (z + t) % NZ
        mover.got(wg.at[:, :, down], ZW + 2 * (t - 1))
        mover.got(wg.at[:, :, up], ZW + 2 * (t - 1) + 1)
        return down, up

    def o_got(t):
        down, up = (z + 8 - t) % NZ, (z + t) % NZ
        mover.got(wog.at[:, down], ZO + 2 * (t - 1))
        mover.got(wog.at[:, up], ZO + 2 * (t - 1) + 1)
        return down, up

    z_step(1, z, z)

    def spread(slot, k):
        shard = xg.at[:, slot]
        mover.put(shard, shard, B1U + k, b_up)
        mover.put(shard, shard, B1D + k, b_down)
        mover.put(shard, shard, TWIN + k, twin)

    from_down, from_up, far = slot_at(a + 3, b), slot_at(a + 1, b), slot_at(a + 2, b)
    mover.got(xg.at[:, from_down], A1)
    mover.put(xg.at[0, from_down], xg.at[0, from_down], A2, a_up)
    spread(from_down, 1)
    mover.got(xg.at[:, from_up], A1 + 1)
    mover.put(xg.at[1, from_up], xg.at[1, from_up], A2 + 1, a_down)
    spread(from_up, 2)
    local[2].wait()
    mover.got(xg.at[0, far], A2)
    mover.got(xg.at[1, far], A2 + 1)
    spread(far, 3)

    def second(k, first):
        down, up = slot_at(first, b + 3), slot_at(first, b + 1)
        mover.got(xg.at[:, down], B1U + k)
        mover.put(xg.at[0, down], xg.at[0, down], B2U + k, b_up)
        mover.put(xg.at[:, down], xg.at[:, down], TWIN + 4 + k, twin)
        mover.got(xg.at[:, up], B1D + k)
        mover.put(xg.at[1, up], xg.at[1, up], B2D + k, b_down)
        mover.put(xg.at[:, up], xg.at[:, up], TWIN + 8 + k, twin)

    def second_far(k, first):
        opposite = slot_at(first, b + 2)
        mover.got(xg.at[0, opposite], B2U + k)
        mover.got(xg.at[1, opposite], B2D + k)
        mover.put(xg.at[:, opposite], xg.at[:, opposite], TWIN + 12 + k, twin)

    second(0, a)
    down, up = z_got(1)
    z_step(2, down, up)
    second(1, a + 3)
    second(2, a + 1)
    down, up = z_got(2)
    z_step(3, down, up)
    second(3, a + 2)
    second_far(0, a)
    down, up = z_got(3)
    z_step(4, down, up)
    o_step(1, z, z)
    second_far(1, a + 3)
    second_far(2, a + 1)
    second_far(3, a + 2)
    opposite = (z + 4) % NZ
    down, up = o_got(1)
    o_step(2, down, up)
    mover.got(wg.at[0, :, opposite], ZW + 6)
    mover.got(wg.at[1, :, opposite], ZW + 7)
    down, up = o_got(2)
    o_step(3, down, up)
    for d in range(1, GROUP):
        mover.got(sgg.at[own_group], s_slot(d))
    for k in range(16):
        mover.got(xg.at[:, own], TWIN + k)
    down, up = o_got(3)
    o_step(4, down, up)
    mover.got(wog.at[0, opposite], ZO + 6)
    mover.got(wog.at[1, opposite], ZO + 7)
    local[1].wait()
    local[3].wait()
    mover.finish()


def project_kernel(x_ref, w_ref, s_ref, gain_ref, keep_ref, y_ref):
    mean_part = jnp.dot(x_ref[0], w_ref[0], preferred_element_type=F32)
    delta_part = jnp.dot(x_ref[1], w_ref[1], preferred_element_type=F32)
    both = (mean_part + s_ref[...].astype(F32) * delta_part).astype(BF16).astype(F32)
    for e in range(2):
        unit = both[:, e * HEAD : (e + 1) * HEAD]
        inverse = lax.rsqrt(jnp.mean(unit * unit, axis=-1, keepdims=True) + EPSILON)
        normed = unit * inverse * gain_ref[e : e + 1, :]
        y_ref[e] = jnp.where(keep_ref[e : e + 1, :] > 0, unit, normed).astype(BF16)


def exchange_kernel(heads, y_ref, kv, q, send, recv, loc):
    x, y, z, c = place()
    me = device(x, y, z, c)
    own = x * 2 + y % 2
    peers = [group_peer(x, y, z, c, d) for d in range(1, GROUP)]
    z_up, z_down = device(x, y, (z + 1) % NZ, c), device(x, y, (z + 7) % NZ, c)
    greet([peer for peer, _ in peers] + [z_up, z_down])
    ref_send, ref_recv = send, recv

    def copy_to(src, dst, s, r, where):
        return pltpu.make_async_remote_copy(
            src_ref=src,
            dst_ref=dst,
            send_sem=ref_send.at[s],
            recv_sem=ref_recv.at[r],
            device_id=where,
            device_id_type=MESH,
        )

    rows = q.shape[2]
    for e in range(2):
        unit = own * 2 + e

        @pl.when(unit < heads)
        def _():
            for d, (peer, there) in enumerate(peers, 1):
                copy_to(
                    y_ref.at[e, pl.ds(there * rows, rows)], q.at[z, unit], e * 7 + d - 1, unit, peer
                ).start()
            pltpu.make_async_copy(
                y_ref.at[e, pl.ds(own * rows, rows)], q.at[z, unit], loc.at[e]
            ).start()

        @pl.when((unit >= heads) & (unit < 3 * heads))
        def _():
            for d, (peer, there) in enumerate(peers, 1):
                copy_to(y_ref.at[e], kv.at[unit - heads], e * 7 + d - 1, unit, peer).start()
            pltpu.make_async_copy(y_ref.at[e], kv.at[unit - heads], loc.at[e]).start()

    for n in range(heads):
        landed = q.at[z, n]

        @pl.when(own == n // 2)
        def _():
            pltpu.make_async_copy(y_ref.at[n % 2, pl.ds(own * rows, rows)], landed, loc.at[n % 2]).wait()

        @pl.when(own != n // 2)
        def _():
            copy_to(landed, landed, 0, n, me).wait_recv()

    Z = 3 * heads
    ring = []
    for t in range(1, 5):
        down, up = (z + 8 - (t - 1)) % NZ, (z + t - 1) % NZ
        if t > 1:
            copy_to(q.at[down], q.at[down], 0, Z + 2 * (t - 2), me).wait_recv()
            copy_to(q.at[up], q.at[up], 0, Z + 2 * (t - 2) + 1, me).wait_recv()
        if t < 4:
            ring.append(copy_to(q.at[down], q.at[down], 14 + 2 * (t - 1), Z + 2 * (t - 1), z_up))
            ring.append(copy_to(q.at[up], q.at[up], 15 + 2 * (t - 1), Z + 2 * (t - 1) + 1, z_down))
        else:
            cut = (heads + 1) // 2
            lower, upper = pl.ds(0, cut), pl.ds(cut, heads - cut)
            ring.append(copy_to(q.at[down, lower], q.at[down, lower], 20, Z + 6, z_up))
            ring.append(copy_to(q.at[up, upper], q.at[up, upper], 21, Z + 7, z_down))
        ring[-2].start()
        ring[-1].start()
    for n in range(heads, 3 * heads):
        landed = kv.at[n - heads]

        @pl.when(own == n // 2)
        def _():
            pltpu.make_async_copy(y_ref.at[n % 2], landed, loc.at[n % 2]).wait()

        @pl.when(own != n // 2)
        def _():
            copy_to(landed, landed, 0, n, me).wait_recv()

    cut = (heads + 1) // 2
    far = (z + 4) % NZ
    lower, upper = pl.ds(0, cut), pl.ds(cut, heads - cut)
    copy_to(q.at[far, lower], q.at[far, lower], 0, Z + 6, me).wait_recv()
    copy_to(q.at[far, upper], q.at[far, upper], 0, Z + 7, me).wait_recv()
    for copy in ring:
        copy.wait_send()
    for e in range(2):
        unit = own * 2 + e

        @pl.when(unit < heads)
        def _():
            for d, (peer, there) in enumerate(peers, 1):
                copy_to(
                    y_ref.at[e, pl.ds(there * rows, rows)], q.at[z, unit], e * 7 + d - 1, unit, peer
                ).wait_send()

        @pl.when((unit >= heads) & (unit < 3 * heads))
        def _():
            for d, (peer, there) in enumerate(peers, 1):
                copy_to(y_ref.at[e], kv.at[unit - heads], e * 7 + d - 1, unit, peer).wait_send()


def attend_kernel(heads, factor, q_ref, k_ref, v_ref, o_ref):
    head = pl.program_id(0)
    planes, rows = q_ref.shape[0], q_ref.shape[2]
    key_block = k_ref[0]
    values = jnp.concatenate([v_ref[0], jnp.ones_like(v_ref[0])], axis=1)
    lane = lax.broadcasted_iota(jnp.int32, (rows, HEAD), 1)

    @pl.when(head == 0)
    def _():
        o_ref[:, :, heads * HEAD :] = jnp.zeros((planes, rows, HEAD), BF16)

    for p in range(planes):
        scores = lax.dot_general(
            q_ref[p, 0], key_block, (((1,), (1,)), ((), ())), preferred_element_type=F32
        )
        weights = jnp.exp2(scores * factor).astype(BF16)
        sums = jnp.dot(weights, values, preferred_element_type=F32)
        o_ref[p, :, pl.ds(pl.multiple_of(head * HEAD, HEAD), HEAD)] = sums[:, :HEAD].astype(BF16)
        held = o_ref[p, :, heads * HEAD :].astype(F32)
        o_ref[p, :, heads * HEAD :] = jnp.where(lane == head, sums[:, HEAD:], held).astype(BF16)


def z_scatter_kernel(part, out, send, recv, loc):
    x, y, z, c = place()
    peers = [(device(x, y, (z + d) % NZ, c), (z + d) % NZ) for d in range(1, NZ)]
    greet([peer for peer, _ in peers])
    mover = Mover(send, recv, device(x, y, z, c))
    local = pltpu.make_async_copy(part.at[z], out.at[z], loc.at[0])
    local.start()
    for d, (peer, there) in enumerate(peers, 1):
        mover.put(part.at[there], out.at[z], d - 1, peer)
    for d in range(1, NZ):
        mover.got(out.at[z], d - 1)
    local.wait()
    mover.finish()


def group_gather_kernel(rows_ref, out, send, recv, loc):
    x, y, z, c = place()
    own = x * 2 + y % 2
    peers = [group_peer(x, y, z, c, d) for d in range(1, GROUP)]
    greet([peer for peer, _ in peers])
    mover = Mover(send, recv, device(x, y, z, c))
    local = pltpu.make_async_copy(rows_ref, out.at[:, own], loc.at[0])
    local.start()
    for d, (peer, there) in enumerate(peers, 1):
        mover.put(rows_ref, out.at[:, own], d - 1, peer)
    for d in range(1, GROUP):
        mover.got(out.at[:, own], d - 1)
    local.wait()
    mover.finish()


def out_kernel(a_ref, w_ref, o_ref):
    for m in range(2):
        o_ref[m] = lax.dot_general(
            a_ref[m], w_ref[m], (((1,), (1,)), ((), ())), preferred_element_type=F32
        ).astype(BF16)


def owner_scatter_kernel(part, out, send, recv, loc):
    x, y, z, c = place()
    own = row_slot(x, y, c)
    count = NX * NY * NC
    peers = []
    for d in range(1, count):
        there = (own + d) % count
        peers.append(
            (device(there // 8, ((there // 2) % 2) * 2 + (there // 4) % 2, z, there % 2), there)
        )
    greet([peer for peer, _ in peers])
    mover = Mover(send, recv, device(x, y, z, c))
    local = pltpu.make_async_copy(part.at[:, own], out.at[:, own], loc.at[0])
    local.start()
    for d, (peer, there) in enumerate(peers, 1):
        mover.put(part.at[:, there], out.at[:, own], d - 1, peer)
    for d in range(1, count):
        mover.got(out.at[:, own], d - 1)
    local.wait()
    mover.finish()


def vmem(count):
    return [pl.BlockSpec(memory_space=pltpu.VMEM)] * count


def body(
    tokens, in_bits, qkv_weights, qkv_bits, gain_query, gain_key, out_weights, mix_bits, out_bits
):
    own_rows, width = tokens.shape
    depth, columns = qkv_weights.shape[2], qkv_weights.shape[3]
    heads = columns // HEAD
    rows = qkv_bits.shape[0]
    plane_rows = rows * GROUP
    blk, uly = lax.axis_index("blk"), lax.axis_index("uly")
    group = (blk // 16) * 2 + blk % 2

    flipped = (tokens.astype(F32) * signed(in_bits)).astype(BF16)
    shard = jnp.stack([tokens, flipped])
    units = jnp.transpose(qkv_weights.reshape(2, 3, depth, heads, HEAD), (1, 3, 0, 2, 4))
    units = units.reshape(3 * heads, 2, depth, HEAD)
    units = jnp.concatenate([units, units[-1:]])
    wj = jnp.transpose(units.reshape(GROUP, 2, 2, depth, HEAD), (0, 2, 3, 1, 4))
    wj = wj.reshape(GROUP, 2, depth, 2 * HEAD)
    wo = jnp.transpose(out_weights, (0, 2, 1))
    signs = signed(qkv_bits).astype(BF16).reshape(rows, 3 * heads * HEAD)
    signs = jnp.concatenate([signs, signs[:, -HEAD:]], axis=1)
    signs = jnp.transpose(signs.reshape(rows, GROUP, 2 * HEAD), (1, 0, 2))

    xg, wg, wog, sgg = comm(
        gather_kernel,
        (shard, wj, wo, signs),
        [
            jax.ShapeDtypeStruct((2, NX * NY * NC, own_rows, width), BF16),
            jax.ShapeDtypeStruct((2, NX, NZ, 2, depth, 2 * HEAD), BF16),
            jax.ShapeDtypeStruct((2, NZ) + wo.shape[1:], BF16),
            jax.ShapeDtypeStruct((GROUP, rows, 2 * HEAD), BF16),
        ],
        66,
        66,
        4,
        0,
    )

    gains = jnp.concatenate(
        [gain_query.reshape(heads, HEAD), gain_key.reshape(heads, HEAD), jnp.ones((heads + 1, HEAD), F32)]
    )
    gain = lax.dynamic_slice_in_dim(gains, group * 2, 2, 0)
    keep = (group * 2 + jnp.arange(2) >= 2 * heads).astype(F32)[:, None] * jnp.ones((1, HEAD), F32)

    step = 128
    y = pl.pallas_call(
        project_kernel,
        grid=(plane_rows // step,),
        out_shape=jax.ShapeDtypeStruct((2, plane_rows, HEAD), BF16),
        in_specs=[
            pl.BlockSpec((2, step, width), lambda i: (0, i, 0)),
            pl.BlockSpec((2, width, 2 * HEAD), lambda i: (0, 0, 0)),
            pl.BlockSpec((step, 2 * HEAD), lambda i: (i, 0)),
            pl.BlockSpec((2, HEAD), lambda i: (0, 0)),
            pl.BlockSpec((2, HEAD), lambda i: (0, 0)),
        ],
        out_specs=pl.BlockSpec((2, step, HEAD), lambda i: (0, i, 0)),
        compiler_params=pltpu.CompilerParams(vmem_limit_bytes=40 << 20),
    )(
        xg.reshape(2, plane_rows, width),
        wg.reshape(2, width, 2 * HEAD),
        sgg.reshape(plane_rows, 2 * HEAD),
        gain,
        keep,
    )

    kv, q = comm(
        functools.partial(exchange_kernel, heads),
        (y,),
        [
            jax.ShapeDtypeStruct((2 * heads, plane_rows, HEAD), BF16),
            jax.ShapeDtypeStruct((NZ, heads, rows, HEAD), BF16),
        ],
        22,
        3 * heads + 8,
        2,
        1,
    )

    packed = (heads + 1) * HEAD
    part = pl.pallas_call(
        functools.partial(attend_kernel, heads, math.log2(math.e) / math.sqrt(HEAD)),
        grid=(heads,),
        out_shape=jax.ShapeDtypeStruct((NZ, rows, packed), BF16),
        in_specs=[
            pl.BlockSpec((NZ, 1, rows, HEAD), lambda i: (0, i, 0, 0)),
            pl.BlockSpec((1, plane_rows, HEAD), lambda i: (i, 0, 0)),
            pl.BlockSpec((1, plane_rows, HEAD), lambda i: (i + heads, 0, 0)),
        ],
        out_specs=pl.BlockSpec((NZ, rows, packed), lambda i: (0, 0, 0)),
        compiler_params=pltpu.CompilerParams(vmem_limit_bytes=40 << 20),
    )(q, kv, kv)

    (parts,) = comm(z_scatter_kernel, (part,), [jax.ShapeDtypeStruct(part.shape, BF16)], 7, 7, 1, 2)
    sums = jnp.sum(parts.astype(F32), axis=0)
    numerator = sums[:, : heads * HEAD].reshape(rows, heads, HEAD)
    denominator = sums[:, heads * HEAD : heads * HEAD + heads]
    attended = (numerator / denominator[:, :, None]).astype(BF16).reshape(rows, heads * HEAD)
    attended_flipped = (attended.astype(F32) * signed(mix_bits)).astype(BF16)
    pair = jnp.stack([attended, attended_flipped])

    (pairs,) = comm(
        group_gather_kernel,
        (pair,),
        [jax.ShapeDtypeStruct((2, GROUP) + pair.shape[1:], BF16)],
        7,
        7,
        1,
        3,
    )
    out_columns = NZ * wo.shape[1]
    partial_out = pl.pallas_call(
        out_kernel,
        out_shape=jax.ShapeDtypeStruct((2, plane_rows, out_columns), BF16),
        in_specs=vmem(2),
        out_specs=pl.BlockSpec(memory_space=pltpu.VMEM),
        compiler_params=pltpu.CompilerParams(vmem_limit_bytes=40 << 20),
    )(pairs.reshape(2, plane_rows, columns), wog.reshape(2, out_columns, columns))

    count = NX * NY * NC
    (landed,) = comm(
        owner_scatter_kernel,
        (partial_out.reshape(2, count, own_rows, out_columns),),
        [jax.ShapeDtypeStruct((2, count, own_rows, out_columns), BF16)],
        count - 1,
        count - 1,
        1,
        4,
    )
    summed = jnp.sum(landed.astype(F32).reshape(2, GROUP, 4, own_rows, out_columns), axis=2)
    summed = summed.reshape(2, NX, 2, own_rows, NZ, out_columns // NZ)
    summed = jnp.transpose(summed, (0, 3, 1, 4, 2, 5)).reshape(2, own_rows, width)
    own_bits = lax.dynamic_slice_in_dim(out_bits, uly * own_rows, own_rows, 0)
    return (summed[0] + signed(own_bits) * summed[1]).astype(BF16)


def solution(mesh):
    return jax.shard_map(
        body,
        mesh=mesh,
        in_specs=(
            P(("blk", "uly"), None),
            P(("blk", "uly"), None),
            P(None, None, "blk", "uly"),
            P("blk", None, "uly"),
            P("uly"),
            P("uly"),
            P(None, "uly", "blk"),
            P("blk", "uly"),
            P("blk", None),
        ),
        out_specs=P(("blk", "uly"), None),
        check_vma=False,
    )
```

time: 1440 us -> 224 us (0.16)
  the two profiles are of different devices: /device:TPU:1 before, /device:TPU:61 now
where the time goes in v1:
time: 224 us; the launch traced here: 223 us
  Pallas kernels  194 us (87%)
  local copies, waits for them, and re-layouts  20.8 us (9%)
  other arithmetic  8.4 us (4%)
    pallas_call x5, Pallas kernels, comm(): pl.pallas_call(kernel, out_shape=outs, in_specs=[pl.BlockSpec(memory_spac...  183 us
    unnamed x28, local copies, waits for them, and re-layouts  13.1 us
    pallas_call x1, Pallas kernels, body(): pl.pallas_call(functools.partial(attend_kernel, heads, math.log2(math.e)...  5.82 us

profile of v1, /device:TPU:61, one launch (start us, length us, event | category | flops | bytes accessed | tf_op | source)
XLA Modules:
  0.0 223.4 jit_solution(17418542506483840830)
XLA Ops:
  0.0 1.1 fusion.2
  1.1 1.6 pad_maximum_fusion.2.xs
  2.7 0.0 copy-start.10
  2.7 1.4 reshape.73
  4.2 0.8 copy.24
  5.0 0.0 copy-done.10
  5.0 0.1 fusion
  5.1 0.0 copy-start.12
  5.1 0.0 copy-start.13
  5.2 0.8 copy.23
  6.0 55.1 %shard_map.91 = (bf16[2,32,24,2560]{3,2,1,0:T(8,128)(2,1)}, bf16[2,4,8,2,40,256]{5,4,3,2,1,0:T(8,128)(2,1)}, bf16[2,8,40,640]{3,2,1,0:T(8,128)(2,1)}, bf16[8,96,256]{2,1,0:T(8,128)(2,1)}) custom-call(bf16[2,24,2560]{2,1,0:T(8,128)(2,1)} %pad_maximum_fusion.2.xs, bf16[8,2,40,256]{3,2,1,0:T(8,128)(2,1)} %bitcast.57, bf16[2,40,640]{2,1,0:T(8,128)(2,1)} %bitcast.62, ...), custom_call_target="tpu_custom_call" | custom-call | tf_op jit(solution)/shard_map/pallas_call | solution.py:81
  61.2 0.1 pad_dynamic-slice_fusion.2
  61.3 0.0 copy-done.12
  61.3 0.0 copy-done.13
  61.3 0.1 fusion.5.gain_ref
  61.3 0.1 mul.48.keep_ref
  61.4 0.0 copy-start
  61.4 3.2 %copy-done = bf16[2,32,24,2560]{3,2,1,0:T(8,128)(2,1)S(1)} copy-done((bf16[2,32,24,2560]{3,2,1,0:T(8,128)(2,1)S(1)}, bf16[2,32,24,2560]{3,2,1,0:T(8,128)(2,1)}, u32[]{:S(2)}) %copy-start) | copy-done | bytes 7864344
  64.6 0.0 copy-start.5
  64.6 1.7 copy-done.5
  66.4 0.0 copy-start.9
  66.4 1.0 copy-done.9
  67.4 4.3 %shard_map.92.y_ref = bf16[2,768,128]{2,1,0:T(8,128)(2,1)S(1)} custom-call(bf16[2,768,2560]{2,1,0:T(8,128)(2,1)S(1)} %bitcast.42, bf16[2,2560,256]{2,1,0:T(8,128)(2,1)S(1)} %bitcast.45, bf16[768,256]{1,0:T(8,128)(2,1)S(1)} %bitcast.47, f32[2,128]{1,0:T(2,128)S(1)} %fusion.5.gain_ref, f32[2,128]{1,0:T(2,128)S(1)} %mul.48.keep_ref), custom_call_target="tpu_custom_call" | custom-call | tf_op jit(solution)/shard_map/pallas_call | solution.py:496
  71.7 0.0 copy-start.6
  71.7 0.7 copy-done.6
  72.4 33.4 %shard_map.93 = (bf16[10,768,128]{2,1,0:T(8,128)(2,1)}, bf16[8,5,96,128]{3,2,1,0:T(8,128)(2,1)}) custom-call(bf16[2,768,128]{2,1,0:T(8,128)(2,1)} %copy-done.6), custom_call_target="tpu_custom_call" | custom-call | tf_op jit(solution)/shard_map/pallas_call | solution.py:81
  105.8 0.0 copy-start.1
  105.9 1.5 copy-done.1
  107.4 0.0 copy-start.7
  107.4 1.2 copy-done.7
  108.6 5.8 %shard_map.94.part = bf16[8,96,768]{2,1,0:T(8,128)(2,1)S(1)} custom-call(bf16[8,5,96,128]{3,2,1,0:T(8,128)(2,1)S(1)} %copy-done.7, bf16[10,768,128]{2,1,0:T(8,128)(2,1)S(1)} %copy-done.1, bf16[10,768,128]{2,1,0:T(8,128)(2,1)S(1)} %copy-done.1), custom_call_target="tpu_custom_call" | custom-call | tf_op jit(solution)/shard_map/pallas_call | solution.py:531
  114.4 0.0 copy-start.3
  114.4 1.0 copy-done.3
  115.4 28.4 %shard_map.95 = bf16[8,96,768]{2,1,0:T(8,128)(2,1)} custom-call(bf16[8,96,768]{2,1,0:T(8,128)(2,1)} %copy-done.3), custom_call_target="tpu_custom_call" | custom-call | tf_op jit(solution)/shard_map/pallas_call | solution.py:81
  143.8 0.0 copy-start.11
  143.8 1.5 convert_reduce_fusion.1
  145.4 0.1 copy.14
  145.5 0.2 copy.15
  145.6 0.0 copy-done.11
  145.6 0.1 fusion.3
  145.7 0.0 copy-start.8
  145.7 0.7 pad_maximum_fusion.3.rows_ref
  146.5 39.7 %shard_map.96 = bf16[2,8,96,640]{3,2,1,0:T(8,128)(2,1)} custom-call(bf16[2,96,640]{2,1,0:T(8,128)(2,1)} %pad_maximum_fusion.3.rows_ref), custom_call_target="tpu_custom_call" | custom-call | tf_op jit(solution)/shard_map/pallas_call | solution.py:81
  186.1 0.0 copy-done.8
  186.1 0.0 copy-start.2
  186.2 1.5 copy-done.2
  187.7 1.3 shard_map.97
  189.0 0.0 copy-start.4
  189.0 1.0 copy-done.4
  190.0 25.9 %shard_map.98 = bf16[2,32,24,320]{3,2,1,0:T(8,128)(2,1)} custom-call(bf16[2,32,24,320]{3,2,1,0:T(8,128)(2,1)} %bitcast.44), custom_call_target="tpu_custom_call" | custom-call | tf_op jit(solution)/shard_map/pallas_call | solution.py:81
  215.9 1.5 convert_reduce_fusion
  217.5 0.6 reshape.89
  218.1 0.1 fusion.7
  218.2 0.6 copy.16
  218.8 1.1 squeeze.6
  220.0 0.6 copy.17
  220.6 1.1 squeeze.7
  221.7 1.6 add_convert_fusion
  (10 shorter events, 0.2 us)
Async XLA Ops:
  2.7 2.3 %copy-start.10 = (s32[96,3,640]{2,0,1:T(8,128)S(1)}, s32[96,3,640]{2,0,1:T(8,128)}, u32[]{:S(2)}) copy-start(s32[96,3,640]{2,0,1:T(8,128)} %param.12) | copy-start | bytes 2211844
  5.1 56.1 %copy-start.12 = (f32[640]{0:T(1024)S(1)}, f32[640]{0:T(1024)}, u32[]{:S(2)}) copy-start(f32[640]{0:T(1024)} %param.13) | copy-start | bytes 7684
  5.1 56.1 %copy-start.13 = (f32[640]{0:T(1024)S(1)}, f32[640]{0:T(1024)}, u32[]{:S(2)}) copy-start(f32[640]{0:T(1024)} %param.14) | copy-start | bytes 7684
  61.4 3.2 %copy-start = (bf16[2,32,24,2560]{3,2,1,0:T(8,128)(2,1)S(1)}, bf16[2,32,24,2560]{3,2,1,0:T(8,128)(2,1)}, u32[]{:S(2)}) copy-start(bf16[2,32,24,2560]{3,2,1,0:T(8,128)(2,1)} %get-tuple-element.11) | copy-start | bytes 23592964
  64.6 1.7 copy-start.5
  66.4 1.0 copy-start.9
  71.7 0.8 copy-start.6
  105.8 1.5 copy-start.1
  107.4 1.2 copy-start.7
  114.4 1.0 copy-start.3
  143.8 1.8 copy-start.11
  145.7 40.4 %copy-start.8 = (bf16[2,8,40,640]{3,2,1,0:T(8,128)(2,1)S(1)}, bf16[2,8,40,640]{3,2,1,0:T(8,128)(2,1)}, u32[]{:S(2)}) copy-start(bf16[2,8,40,640]{3,2,1,0:T(8,128)(2,1)} %get-tuple-element.16) | copy-start | bytes 2457604
  186.1 1.5 copy-start.2
  189.0 1.0 copy-start.4

commit v2 on v1

--- a/solution.py
+++ b/solution.py
@@ -65,16 +65,16 @@
             copy.wait_send()
 
 
-def greet(partners):
+def greet(sources, count):
     barrier = pltpu.get_barrier_semaphore()
-    for partner in partners:
-        pl.semaphore_signal(barrier, inc=1, device_id=partner, device_id_type=MESH)
-    pl.semaphore_wait(barrier, len(partners))
+    for source in sources:
+        pl.semaphore_signal(barrier, inc=1, device_id=source, device_id_type=MESH)
+    pl.semaphore_wait(barrier, count)
 
 
 def group_peer(x, y, z, c, d):
-    there = (x * 2 + y % 2 + d) % GROUP
-    return device(there // 2, (y // 2) * 2 + there % 2, z, c), there
+    there = (x * 2 + c + d) % GROUP
+    return device(there // 2, y, z, there % 2), there
 
 
 def comm(kernel, args, outs, sends, recvs, locals_, collective_id):
@@ -92,11 +92,12 @@
     )(*args)
 
 
-def gather_kernel(xs, wj, wo, sg, xg, wg, wog, sgg, send, recv, loc):
+def gather_kernel(xs, wj, sg, gains, xg, wg, sgg, gg, send, recv, loc):
     x, y, z, c = place()
-    low = y % 2
+    low, high = y % 2, y // 2
     me = device(x, y, z, c)
-    own_group = x * 2 + low
+    group = x * 2 + c
+    chunk = x * 2 + low
     a = x * (1 - c) + y * c
     b = y * (1 - c) + x * c
 
@@ -115,42 +116,88 @@
     b_up, b_down = dev_at(a, b + 1), dev_at(a, b + 3)
     z_up, z_down = device(x, y, (z + 1) % NZ, c), device(x, y, (z + 7) % NZ, c)
     twin = device(x, y, z, 1 - c)
-    peers = [group_peer(x, y, z, c, d) for d in range(1, GROUP)]
-    other_y = device(x, (y + 3 + 2 * (y % 2)) % 4, z, c)
-    greet([peer for peer, _ in peers] + [other_y, twin, z_up, z_down])
+    targets = []
+    for d in range(GROUP):
+        there = (group + d) % GROUP
+        targets.append((device(there // 2, high * 2 + c, z, there % 2), there))
+    origins = [device(k // 2, high * 2 + k % 2, z, low) for k in range(GROUP)]
+    stays = low == c
+
+    barrier = pltpu.get_barrier_semaphore()
+    for near in (a_up, a_down, b_up, b_down, z_up, z_down, twin):
+        pl.semaphore_signal(barrier, inc=1, device_id=near, device_id_type=MESH)
+    for k, origin in enumerate(origins):
+
+        @pl.when(jnp.logical_not(stays & (chunk == k)))
+        def _():
+            pl.semaphore_signal(barrier, inc=1, device_id=origin, device_id_type=MESH)
+
+    @pl.when(stays)
+    def _():
+        pl.semaphore_wait(barrier, 7 + GROUP - 1)
+
+    @pl.when(jnp.logical_not(stays))
+    def _():
+        pl.semaphore_wait(barrier, 7 + GROUP)
 
     mover = Mover(send, recv, me)
     own = slot_at(a, b)
-    local = [
-        pltpu.make_async_copy(wj.at[own_group], wg.at[:, x, z, low], loc.at[0]),
-        pltpu.make_async_copy(xs, xg.at[:, own], loc.at[1]),
-        pltpu.make_async_copy(wo, wog.at[:, z], loc.at[2]),
-        pltpu.make_async_copy(sg.at[own_group], sgg.at[own_group], loc.at[3]),
-    ]
-    for copy in local:
-        copy.start()
-
-    def w_slot(d):
-        return d - 1
-
-    def s_slot(d):
-        return 7 + d - 1
-
-    A1, A2, B1U, B1D, B2U, B2D, TWIN, ZW, ZO = 14, 16, 18, 22, 26, 30, 34, 50, 58
-
-    for d, (peer, there) in enumerate(peers, 1):
-        mover.put(wj.at[there], wg.at[:, x, z, low], w_slot(d), peer)
+    A1, A2, B1U, B1D, B2U, B2D, TWIN, ZW, GAIN, SIGN = 8, 10, 12, 16, 20, 24, 28, 44, 52, 53
+    KEPT = 59
+
+    def kept(part, remote):
+        source = wj.at[group] if part == 0 else sg.at[group]
+        landed = wg.at[:, x, z, low] if part == 0 else sgg.at[chunk]
+        if not remote:
+            return pltpu.make_async_copy(source, landed, loc.at[part])
+        return pltpu.make_async_remote_copy(
+            src_ref=source,
+            dst_ref=landed,
+            send_sem=send.at[KEPT + part],
+            recv_sem=recv.at[chunk + SIGN * part],
+            device_id=targets[0][0],
+            device_id_type=MESH,
+        )
+
+    def start_kept(part):
+        @pl.when(stays)
+        def _():
+            kept(part, False).start()
+
+        @pl.when(jnp.logical_not(stays))
+        def _():
+            kept(part, True).start()
+
+    def arrive_all(part, ref):
+        for k in range(GROUP):
+            mine = stays & (chunk == k)
+
+            @pl.when(mine)
+            def _():
+                kept(part, False).wait()
+
+            @pl.when(jnp.logical_not(mine))
+            def _():
+                mover.got(ref, k + SIGN * part)
+
+    start_kept(0)
+    for peer, there in targets[1:]:
+        mover.put(wj.at[there], wg.at[:, x, z, low], chunk, peer)
     mover.put(xs, xg.at[:, own], A1, a_up)
     mover.put(xs, xg.at[:, own], A1 + 1, a_down)
     mover.put(xs, xg.at[:, own], B1U, b_up)
     mover.put(xs, xg.at[:, own], B1D, b_down)
     mover.put(xs, xg.at[:, own], TWIN, twin)
-    for d, (peer, there) in enumerate(peers, 1):
-        mover.put(sg.at[there], sgg.at[own_group], s_slot(d), peer)
-
-    local[0].wait()
-    for d in range(1, GROUP):
-        mover.got(wg.at[:, x, z, low], w_slot(d))
+    mover.put(gains, gg.at[c], GAIN, twin)
+    own_rows = pltpu.make_async_copy(xs, xg.at[:, own], loc.at[2])
+    own_gains = pltpu.make_async_copy(gains, gg.at[c], loc.at[3])
+    own_rows.start()
+    own_gains.start()
+    start_kept(1)
+    for peer, there in targets[1:]:
+        mover.put(sg.at[there], sgg.at[chunk], SIGN + chunk, peer)
+
+    arrive_all(0, wg.at[:, x, z, low])
 
     def z_step(t, source_down, source_up):
         if t < 4:
@@ -160,24 +207,10 @@
             mover.put(wg.at[0, :, source_down], wg.at[0, :, source_down], ZW + 6, z_up)
             mover.put(wg.at[1, :, source_up], wg.at[1, :, source_up], ZW + 7, z_down)
 
-    def o_step(t, source_down, source_up):
-        if t < 4:
-            mover.put(wog.at[:, source_down], wog.at[:, source_down], ZO + 2 * (t - 1), z_up)
-            mover.put(wog.at[:, source_up], wog.at[:, source_up], ZO + 2 * (t - 1) + 1, z_down)
-        else:
-            mover.put(wog.at[0, source_down], wog.at[0, source_down], ZO + 6, z_up)
-            mover.put(wog.at[1, source_up], wog.at[1, source_up], ZO + 7, z_down)
-
     def z_got(t):
         down, up = (z + 8 - t) % NZ, (z + t) % NZ
         mover.got(wg.at[:, :, down], ZW + 2 * (t - 1))
         mover.got(wg.at[:, :, up], ZW + 2 * (t - 1) + 1)
-        return down, up
-
-    def o_got(t):
-        down, up = (z + 8 - t) % NZ, (z + t) % NZ
-        mover.got(wog.at[:, down], ZO + 2 * (t - 1))
-        mover.got(wog.at[:, up], ZO + 2 * (t - 1) + 1)
         return down, up
 
     z_step(1, z, z)
@@ -195,7 +228,6 @@
     mover.got(xg.at[:, from_up], A1 + 1)
     mover.put(xg.at[1, from_up], xg.at[1, from_up], A2 + 1, a_down)
     spread(from_up, 2)
-    local[2].wait()
     mover.got(xg.at[0, far], A2)
     mover.got(xg.at[1, far], A2 + 1)
     spread(far, 3)
@@ -224,30 +256,27 @@
     z_step(3, down, up)
     second(3, a + 2)
     second_far(0, a)
+    second_far(1, a + 3)
     down, up = z_got(3)
     z_step(4, down, up)
-    o_step(1, z, z)
-    second_far(1, a + 3)
     second_far(2, a + 1)
     second_far(3, a + 2)
     opposite = (z + 4) % NZ
-    down, up = o_got(1)
-    o_step(2, down, up)
+    arrive_all(1, sgg.at[chunk])
+    for k in range(16):
+        mover.got(xg.at[:, own], TWIN + k)
+    mover.got(gg.at[c], GAIN)
     mover.got(wg.at[0, :, opposite], ZW + 6)
     mover.got(wg.at[1, :, opposite], ZW + 7)
-    down, up = o_got(2)
-    o_step(3, down, up)
-    for d in range(1, GROUP):
-        mover.got(sgg.at[own_group], s_slot(d))
-    for k in range(16):
-        mover.got(xg.at[:, own], TWIN + k)
-    down, up = o_got(3)
-    o_step(4, down, up)
-    mover.got(wog.at[0, opposite], ZO + 6)
-    mover.got(wog.at[1, opposite], ZO + 7)
-    local[1].wait()
-    local[3].wait()
+    own_rows.wait()
+    own_gains.wait()
+    assert len(mover.sent) == KEPT, len(mover.sent)
     mover.finish()
+
+    @pl.when(jnp.logical_not(stays))
+    def _():
+        for part in range(2):
+            kept(part, True).wait_send()
 
 
 def project_kernel(x_ref, w_ref, s_ref, gain_ref, keep_ref, y_ref):
@@ -261,105 +290,168 @@
         y_ref[e] = jnp.where(keep_ref[e : e + 1, :] > 0, unit, normed).astype(BF16)
 
 
-def exchange_kernel(heads, y_ref, kv, q, send, recv, loc):
+def exchange_kernel(heads, y_ref, mix, wo, kv, q, mixed, wos, send, recv, loc):
     x, y, z, c = place()
+    low, high = y % 2, y // 2
     me = device(x, y, z, c)
-    own = x * 2 + y % 2
+    own = x * 2 + c
+    rows = q.shape[2]
+    units = 3 * heads
     peers = [group_peer(x, y, z, c, d) for d in range(1, GROUP)]
+    aligned = [device((x + d) % NX, y, z, c) for d in range(1, NX)]
+    twin = device(x, y, z, 1 - c)
+    swap = device(x, high * 2 + c, z, low)
     z_up, z_down = device(x, y, (z + 1) % NZ, c), device(x, y, (z + 7) % NZ, c)
-    greet([peer for peer, _ in peers] + [z_up, z_down])
-    ref_send, ref_recv = send, recv
+    moves = low != c
+
+    barrier = pltpu.get_barrier_semaphore()
+    for near in [peer for peer, _ in peers] + [z_up, z_down]:
+        pl.semaphore_signal(barrier, inc=1, device_id=near, device_id_type=MESH)
+
+    @pl.when(moves)
+    def _():
+        pl.semaphore_signal(barrier, inc=1, device_id=swap, device_id_type=MESH)
+        pl.semaphore_wait(barrier, GROUP + 2)
+
+    @pl.when(jnp.logical_not(moves))
+    def _():
+        pl.semaphore_wait(barrier, GROUP + 1)
 
     def copy_to(src, dst, s, r, where):
         return pltpu.make_async_remote_copy(
             src_ref=src,
             dst_ref=dst,
-            send_sem=ref_send.at[s],
-            recv_sem=ref_recv.at[r],
+            send_sem=send.at[s],
+            recv_sem=recv.at[r],
             device_id=where,
             device_id_type=MESH,
         )
 
-    rows = q.shape[2]
-    for e in range(2):
-        unit = own * 2 + e
-
-        @pl.when(unit < heads)
-        def _():
-            for d, (peer, there) in enumerate(peers, 1):
-                copy_to(
-                    y_ref.at[e, pl.ds(there * rows, rows)], q.at[z, unit], e * 7 + d - 1, unit, peer
-                ).start()
-            pltpu.make_async_copy(
-                y_ref.at[e, pl.ds(own * rows, rows)], q.at[z, unit], loc.at[e]
-            ).start()
-
-        @pl.when((unit >= heads) & (unit < 3 * heads))
-        def _():
-            for d, (peer, there) in enumerate(peers, 1):
-                copy_to(y_ref.at[e], kv.at[unit - heads], e * 7 + d - 1, unit, peer).start()
-            pltpu.make_async_copy(y_ref.at[e], kv.at[unit - heads], loc.at[e]).start()
-
-    for n in range(heads):
-        landed = q.at[z, n]
+    RING, FORWARD = 14, 22
+    SWAP = FORWARD + 2 * heads
+    Z, R_SWAP = units, units + 8
+
+    def own_copies(n):
+        e = n % 2
+        if n < heads:
+            return [
+                copy_to(y_ref.at[e, pl.ds(there * rows, rows)], q.at[z, n], e * 7 + d, n, peer)
+                for d, (peer, there) in enumerate(peers)
+            ]
+        landed = kv.at[n - heads]
+        return [
+            copy_to(y_ref.at[e], landed, e * 7 + d, n, peer)
+            for d, peer in enumerate(aligned + [twin])
+        ]
+
+    def kept(n):
+        source = y_ref.at[n % 2]
+        if n < heads:
+            return pltpu.make_async_copy(source.at[pl.ds(own * rows, rows)], q.at[z, n], loc.at[n % 2])
+        return pltpu.make_async_copy(source, kv.at[n - heads], loc.at[n % 2])
+
+    for n in range(units):
 
         @pl.when(own == n // 2)
         def _():
-            pltpu.make_async_copy(y_ref.at[n % 2, pl.ds(own * rows, rows)], landed, loc.at[n % 2]).wait()
+            for copy in own_copies(n):
+                copy.start()
+            kept(n).start()
+
+    swaps = [copy_to(mix, mixed, SWAP, R_SWAP, swap), copy_to(wo, wos, SWAP + 1, R_SWAP + 1, swap)]
+    stays = [
+        pltpu.make_async_copy(mix, mixed, loc.at[2]),
+        pltpu.make_async_copy(wo, wos, loc.at[3]),
+    ]
+
+    @pl.when(moves)
+    def _():
+        for copy in swaps:
+            copy.start()
+
+    @pl.when(jnp.logical_not(moves))
+    def _():
+        for copy in stays:
+            copy.start()
+
+    def arrive(n):
+        landed = q.at[z, n] if n < heads else kv.at[n - heads]
+
+        @pl.when(own == n // 2)
+        def _():
+            kept(n).wait()
 
         @pl.when(own != n // 2)
         def _():
             copy_to(landed, landed, 0, n, me).wait_recv()
 
-    Z = 3 * heads
+    def forward(n):
+        landed = kv.at[n - heads]
+        return copy_to(landed, landed, FORWARD + n - heads, n, twin)
+
+    def forwards(n):
+        return (own != n // 2) & (c == (n // 2) % 2)
+
+    for n in range(heads):
+        arrive(n)
+
+    cut = (heads + 1) // 2
+    lower, upper = pl.ds(0, cut), pl.ds(cut, heads - cut)
     ring = []
-    for t in range(1, 5):
+
+    def ring_step(t):
         down, up = (z + 8 - (t - 1)) % NZ, (z + t - 1) % NZ
         if t > 1:
             copy_to(q.at[down], q.at[down], 0, Z + 2 * (t - 2), me).wait_recv()
             copy_to(q.at[up], q.at[up], 0, Z + 2 * (t - 2) + 1, me).wait_recv()
+        r, s = Z + 2 * (t - 1), RING + 2 * (t - 1)
         if t < 4:
-            ring.append(copy_to(q.at[down], q.at[down], 14 + 2 * (t - 1), Z + 2 * (t - 1), z_up))
-            ring.append(copy_to(q.at[up], q.at[up], 15 + 2 * (t - 1), Z + 2 * (t - 1) + 1, z_down))
+            ring.append(copy_to(q.at[down], q.at[down], s, r, z_up))
+            ring.append(copy_to(q.at[up], q.at[up], s + 1, r + 1, z_down))
         else:
-            cut = (heads + 1) // 2
-            lower, upper = pl.ds(0, cut), pl.ds(cut, heads - cut)
-            ring.append(copy_to(q.at[down, lower], q.at[down, lower], 20, Z + 6, z_up))
-            ring.append(copy_to(q.at[up, upper], q.at[up, upper], 21, Z + 7, z_down))
+            ring.append(copy_to(q.at[down, lower], q.at[down, lower], s, r, z_up))
+            ring.append(copy_to(q.at[up, upper], q.at[up, upper], s + 1, r + 1, z_down))
         ring[-2].start()
         ring[-1].start()
-    for n in range(heads, 3 * heads):
-        landed = kv.at[n - heads]
-
-        @pl.when(own == n // 2)
-        def _():
-            pltpu.make_async_copy(y_ref.at[n % 2], landed, loc.at[n % 2]).wait()
-
-        @pl.when(own != n // 2)
-        def _():
-            copy_to(landed, landed, 0, n, me).wait_recv()
-
-    cut = (heads + 1) // 2
+
+    ring_step(1)
+    for t in range(2, 5):
+        ring_step(t)
+        for n in range(heads, units):
+            if (n - heads) % 3 == t - 2:
+                arrive(n)
+
+                @pl.when(forwards(n))
+                def _():
+                    forward(n).start()
+
     far = (z + 4) % NZ
-    lower, upper = pl.ds(0, cut), pl.ds(cut, heads - cut)
     copy_to(q.at[far, lower], q.at[far, lower], 0, Z + 6, me).wait_recv()
     copy_to(q.at[far, upper], q.at[far, upper], 0, Z + 7, me).wait_recv()
     for copy in ring:
         copy.wait_send()
-    for e in range(2):
-        unit = own * 2 + e
-
-        @pl.when(unit < heads)
+    for n in range(units):
+
+        @pl.when(own == n // 2)
         def _():
-            for d, (peer, there) in enumerate(peers, 1):
-                copy_to(
-                    y_ref.at[e, pl.ds(there * rows, rows)], q.at[z, unit], e * 7 + d - 1, unit, peer
-                ).wait_send()
-
-        @pl.when((unit >= heads) & (unit < 3 * heads))
-        def _():
-            for d, (peer, there) in enumerate(peers, 1):
-                copy_to(y_ref.at[e], kv.at[unit - heads], e * 7 + d - 1, unit, peer).wait_send()
+            for copy in own_copies(n):
+                copy.wait_send()
+
+        if n >= heads:
+
+            @pl.when(forwards(n))
+            def _():
+                forward(n).wait_send()
+
+    @pl.when(moves)
+    def _():
+        for copy in swaps:
+            copy.wait()
+
+    @pl.when(jnp.logical_not(moves))
+    def _():
+        for copy in stays:
+            copy.wait()
 
 
 def attend_kernel(heads, factor, q_ref, k_ref, v_ref, o_ref):
@@ -387,7 +479,7 @@
 def z_scatter_kernel(part, out, send, recv, loc):
     x, y, z, c = place()
     peers = [(device(x, y, (z + d) % NZ, c), (z + d) % NZ) for d in range(1, NZ)]
-    greet([peer for peer, _ in peers])
+    greet([peer for peer, _ in peers], len(peers))
     mover = Mover(send, recv, device(x, y, z, c))
     local = pltpu.make_async_copy(part.at[z], out.at[z], loc.at[0])
     local.start()
@@ -399,19 +491,54 @@
     mover.finish()
 
 
-def group_gather_kernel(rows_ref, out, send, recv, loc):
+def group_gather_kernel(rows_ref, wo, out, wog, send, recv, loc):
     x, y, z, c = place()
-    own = x * 2 + y % 2
-    peers = [group_peer(x, y, z, c, d) for d in range(1, GROUP)]
-    greet([peer for peer, _ in peers])
+    own = x * 2 + c
+    aligned = [device((x + d) % NX, y, z, c) for d in range(1, NX)]
+    twin = device(x, y, z, 1 - c)
+    z_up, z_down = device(x, y, (z + 1) % NZ, c), device(x, y, (z + 7) % NZ, c)
+    near = aligned + [twin, z_up, z_down]
+    greet(near, len(near))
     mover = Mover(send, recv, device(x, y, z, c))
-    local = pltpu.make_async_copy(rows_ref, out.at[:, own], loc.at[0])
-    local.start()
-    for d, (peer, there) in enumerate(peers, 1):
-        mover.put(rows_ref, out.at[:, own], d - 1, peer)
-    for d in range(1, GROUP):
-        mover.got(out.at[:, own], d - 1)
-    local.wait()
+    local = [
+        pltpu.make_async_copy(rows_ref, out.at[:, own], loc.at[0]),
+        pltpu.make_async_copy(wo, wog.at[:, z], loc.at[1]),
+    ]
+    for copy in local:
+        copy.start()
+    TWIN, ZO = 3, 7
+    for d, peer in enumerate(aligned):
+        mover.put(rows_ref, out.at[:, own], d, peer)
+    mover.put(rows_ref, out.at[:, own], TWIN, twin)
+    mover.put(wo, wog.at[:, z], ZO, z_up)
+    mover.put(wo, wog.at[:, z], ZO + 1, z_down)
+
+    def o_next(t):
+        down, up = (z + 8 - t) % NZ, (z + t) % NZ
+        mover.got(wog.at[:, down], ZO + 2 * (t - 1))
+        mover.got(wog.at[:, up], ZO + 2 * (t - 1) + 1)
+        if t < 3:
+            mover.put(wog.at[:, down], wog.at[:, down], ZO + 2 * t, z_up)
+            mover.put(wog.at[:, up], wog.at[:, up], ZO + 2 * t + 1, z_down)
+        else:
+            mover.put(wog.at[0, down], wog.at[0, down], ZO + 6, z_up)
+            mover.put(wog.at[1, up], wog.at[1, up], ZO + 7, z_down)
+
+    order = (0, 2, 1)
+    o_next(1)
+    for step, d in enumerate(order):
+        there = ((x + NX - 1 - d) % NX) * 2 + c
+        mover.got(out.at[:, there], d)
+        mover.put(out.at[:, there], out.at[:, there], TWIN + 1 + d, twin)
+        if step < 2:
+            o_next(2 + step)
+    far = (z + 4) % NZ
+    mover.got(wog.at[0, far], ZO + 6)
+    mover.got(wog.at[1, far], ZO + 7)
+    for k in range(NX):
+        mover.got(out.at[:, own], TWIN + k)
+    for copy in local:
+        copy.wait()
     mover.finish()
 
 
@@ -425,6 +552,7 @@
 def owner_scatter_kernel(part, out, send, recv, loc):
     x, y, z, c = place()
     own = row_slot(x, y, c)
+    landing = (x * 2 + c) * NY + y
     count = NX * NY * NC
     peers = []
     for d in range(1, count):
@@ -432,14 +560,14 @@
         peers.append(
             (device(there // 8, ((there // 2) % 2) * 2 + (there // 4) % 2, z, there % 2), there)
         )
-    greet([peer for peer, _ in peers])
+    greet([peer for peer, _ in peers], len(peers))
     mover = Mover(send, recv, device(x, y, z, c))
-    local = pltpu.make_async_copy(part.at[:, own], out.at[:, own], loc.at[0])
+    local = pltpu.make_async_copy(part.at[:, own], out.at[:, landing], loc.at[0])
     local.start()
     for d, (peer, there) in enumerate(peers, 1):
-        mover.put(part.at[:, there], out.at[:, own], d - 1, peer)
+        mover.put(part.at[:, there], out.at[:, landing], d - 1, peer)
     for d in range(1, count):
-        mover.got(out.at[:, own], d - 1)
+        mover.got(out.at[:, landing], d - 1)
     local.wait()
     mover.finish()
 
@@ -456,8 +584,8 @@
     heads = columns // HEAD
     rows = qkv_bits.shape[0]
     plane_rows = rows * GROUP
-    blk, uly = lax.axis_index("blk"), lax.axis_index("uly")
-    group = (blk // 16) * 2 + blk % 2
+    x, y, _, c = place()
+    group = x * 2 + c
 
     flipped = (tokens.astype(F32) * signed(in_bits)).astype(BF16)
     shard = jnp.stack([tokens, flipped])
@@ -471,29 +599,30 @@
     signs = jnp.concatenate([signs, signs[:, -HEAD:]], axis=1)
     signs = jnp.transpose(signs.reshape(rows, GROUP, 2 * HEAD), (1, 0, 2))
 
-    xg, wg, wog, sgg = comm(
+    gains = jnp.stack([gain_query.reshape(heads, HEAD), gain_key.reshape(heads, HEAD)])
+
+    xg, wg, sgg, gg = comm(
         gather_kernel,
-        (shard, wj, wo, signs),
+        (shard, wj, signs, gains),
         [
             jax.ShapeDtypeStruct((2, NX * NY * NC, own_rows, width), BF16),
             jax.ShapeDtypeStruct((2, NX, NZ, 2, depth, 2 * HEAD), BF16),
-            jax.ShapeDtypeStruct((2, NZ) + wo.shape[1:], BF16),
             jax.ShapeDtypeStruct((GROUP, rows, 2 * HEAD), BF16),
+            jax.ShapeDtypeStruct((2,) + gains.shape, F32),
         ],
-        66,
-        66,
+        61,
+        61,
         4,
         0,
     )
 
-    gains = jnp.concatenate(
-        [gain_query.reshape(heads, HEAD), gain_key.reshape(heads, HEAD), jnp.ones((heads + 1, HEAD), F32)]
-    )
+    gains = lax.dynamic_index_in_dim(gg, y % 2, 0, keepdims=False).reshape(2 * heads, HEAD)
+    gains = jnp.concatenate([gains, jnp.ones((heads + 1, HEAD), F32)])
     gain = lax.dynamic_slice_in_dim(gains, group * 2, 2, 0)
     keep = (group * 2 + jnp.arange(2) >= 2 * heads).astype(F32)[:, None] * jnp.ones((1, HEAD), F32)
 
     step = 128
-    y = pl.pallas_call(
+    units = pl.pallas_call(
         project_kernel,
         grid=(plane_rows // step,),
         out_shape=jax.ShapeDtypeStruct((2, plane_rows, HEAD), BF16),
@@ -514,16 +643,19 @@
         keep,
     )
 
-    kv, q = comm(
+    mix = signed(mix_bits).astype(BF16)
+    kv, q, mixed, wo = comm(
         functools.partial(exchange_kernel, heads),
-        (y,),
+        (units, mix, wo),
         [
             jax.ShapeDtypeStruct((2 * heads, plane_rows, HEAD), BF16),
             jax.ShapeDtypeStruct((NZ, heads, rows, HEAD), BF16),
+            jax.ShapeDtypeStruct(mix.shape, BF16),
+            jax.ShapeDtypeStruct(wo.shape, BF16),
         ],
-        22,
-        3 * heads + 8,
-        2,
+        24 + 2 * heads,
+        3 * heads + 10,
+        4,
         1,
     )
 
@@ -546,16 +678,19 @@
     numerator = sums[:, : heads * HEAD].reshape(rows, heads, HEAD)
     denominator = sums[:, heads * HEAD : heads * HEAD + heads]
     attended = (numerator / denominator[:, :, None]).astype(BF16).reshape(rows, heads * HEAD)
-    attended_flipped = (attended.astype(F32) * signed(mix_bits)).astype(BF16)
+    attended_flipped = (attended.astype(F32) * mixed.astype(F32)).astype(BF16)
     pair = jnp.stack([attended, attended_flipped])
 
-    (pairs,) = comm(
+    pairs, wog = comm(
         group_gather_kernel,
-        (pair,),
-        [jax.ShapeDtypeStruct((2, GROUP) + pair.shape[1:], BF16)],
-        7,
-        7,
-        1,
+        (pair, wo),
+        [
+            jax.ShapeDtypeStruct((2, GROUP) + pair.shape[1:], BF16),
+            jax.ShapeDtypeStruct((2, NZ) + wo.shape[1:], BF16),
+        ],
+        15,
+        15,
+        2,
         3,
     )
     out_columns = NZ * wo.shape[1]
@@ -580,7 +715,7 @@
     summed = jnp.sum(landed.astype(F32).reshape(2, GROUP, 4, own_rows, out_columns), axis=2)
     summed = summed.reshape(2, NX, 2, own_rows, NZ, out_columns // NZ)
     summed = jnp.transpose(summed, (0, 3, 1, 4, 2, 5)).reshape(2, own_rows, width)
-    own_bits = lax.dynamic_slice_in_dim(out_bits, uly * own_rows, own_rows, 0)
+    own_bits = lax.dynamic_slice_in_dim(out_bits, lax.axis_index("uly") * own_rows, own_rows, 0)
     return (summed[0] + signed(own_bits) * summed[1]).astype(BF16)
 
 

time: 224 us -> 206 us (0.920)
  the two profiles are of different devices: /device:TPU:61 before, /device:TPU:1 now
where the time goes in v2:
time: 206 us; the launch traced here: 202 us
  Pallas kernels  170 us (83%)
  local copies, waits for them, and re-layouts  22.5 us (11%)
  other arithmetic  9.58 us (5%)
    pallas_call x5, Pallas kernels, comm(): pl.pallas_call(kernel, out_shape=outs, in_specs=[pl.BlockSpec(memory_spac...  158 us
    unnamed x30, local copies, waits for them, and re-layouts  14.2 us
    pallas_call x1, Pallas kernels, body(): pl.pallas_call(functools.partial(attend_kernel, heads, math.log2(math.e)...  5.82 us
    pallas_call x1, Pallas kernels, body(): pl.pallas_call(project_kernel, grid=(plane_rows // step,), out_shape=jax....  4.26 us

profile of v2, /device:TPU:1, one launch (start us, length us, event | category | flops | bytes accessed | tf_op | source)
XLA Modules:
  0.0 202.2 jit_solution(11461957320877998918)
XLA Ops:
  0.0 1.1 fusion.2
  1.1 1.6 pad_maximum_fusion.2.xs
  2.7 0.0 copy-start.10
  2.7 1.4 reshape.71
  4.2 0.8 copy.24
  5.0 0.0 copy-done.10
  5.0 0.0 copy-start.13
  5.0 0.0 copy-start.14
  5.0 0.1 fusion
  5.2 0.8 copy.23
  6.0 0.0 copy-done.13
  6.0 0.0 copy-done.14
  6.0 0.6 pad_maximum_fusion.4.gains
  6.6 49.2 %shard_map.91 = (bf16[2,32,24,2560]{3,2,1,0:T(8,128)(2,1)}, bf16[2,4,8,2,40,256]{5,4,3,2,1,0:T(8,128)(2,1)}, bf16[8,96,256]{2,1,0:T(8,128)(2,1)}, f32[2,2,5,128]{3,2,1,0:T(8,128)}) custom-call(bf16[2,24,2560]{2,1,0:T(8,128)(2,1)} %pad_maximum_fusion.2.xs, bf16[8,2,40,256]{3,2,1,0:T(8,128)(2,1)} %bitcast.59, bf16[8,96,256]{2,1,0:T(8,128)(2,1)} %bitcast.54, ...), custom_call_target="tpu_custom_call" | custom-call | tf_op jit(solution)/shard_map/pallas_call | solution.py:81
  55.8 0.7 constant_dynamic-slice_fusion
  56.6 0.1 mul.52.keep_ref
  56.6 0.0 copy-start
  56.6 3.2 %copy-done = bf16[2,32,24,2560]{3,2,1,0:T(8,128)(2,1)S(1)} copy-done((bf16[2,32,24,2560]{3,2,1,0:T(8,128)(2,1)S(1)}, bf16[2,32,24,2560]{3,2,1,0:T(8,128)(2,1)}, u32[]{:S(2)}) %copy-start) | copy-done | bytes 7864344
  59.9 0.0 copy-start.4
  59.9 1.7 copy-done.4
  61.6 0.0 copy-start.9
  61.6 1.0 copy-done.9
  62.6 0.0 copy-start.11
  62.6 4.3 %shard_map.92.y_ref = bf16[2,768,128]{2,1,0:T(8,128)(2,1)S(1)} custom-call(bf16[2,768,2560]{2,1,0:T(8,128)(2,1)S(1)} %bitcast.42, bf16[2,2560,256]{2,1,0:T(8,128)(2,1)S(1)} %bitcast.44, bf16[768,256]{1,0:T(8,128)(2,1)S(1)} %bitcast.47, f32[2,128]{1,0:T(2,128)S(1)} %pad_dynamic-slice_fusion.gain_ref, f32[2,128]{1,0:T(2,128)S(1)} %mul.52.keep_ref), custom_call_target="tpu_custom_call" | custom-call | tf_op jit(solution)/shard_map/pallas_call | solution.py:625
  66.9 0.0 copy-start.6
  66.9 0.7 copy-done.6
  67.6 0.0 copy-done.11
  67.6 0.7 convert_convert_fusion.1.mix
  68.3 35.0 %shard_map.93 = (bf16[10,768,128]{2,1,0:T(8,128)(2,1)}, bf16[8,5,96,128]{3,2,1,0:T(8,128)(2,1)}, bf16[96,640]{1,0:T(8,128)(2,1)}, bf16[2,40,640]{2,1,0:T(8,128)(2,1)}) custom-call(bf16[2,768,128]{2,1,0:T(8,128)(2,1)} %copy-done.6, bf16[96,640]{1,0:T(8,128)(2,1)} %convert_convert_fusion.1.mix, bf16[2,40,640]{2,1,0:T(8,128)(2,1)} %bitcast.62), custom_call_target="tpu_custom_call" | custom-call | tf_op jit(solution)/shard_map/pallas_call | solution.py:81
  103.4 0.0 copy-start.1
  103.4 1.5 copy-done.1
  104.9 0.0 copy-start.7
  104.9 1.2 copy-done.7
  106.1 5.8 %shard_map.94.part = bf16[8,96,768]{2,1,0:T(8,128)(2,1)S(1)} custom-call(bf16[8,5,96,128]{3,2,1,0:T(8,128)(2,1)S(1)} %copy-done.7, bf16[10,768,128]{2,1,0:T(8,128)(2,1)S(1)} %copy-done.1, bf16[10,768,128]{2,1,0:T(8,128)(2,1)S(1)} %copy-done.1), custom_call_target="tpu_custom_call" | custom-call | tf_op jit(solution)/shard_map/pallas_call | solution.py:663
  111.9 0.0 copy-start.2
  111.9 1.0 copy-done.2
  113.0 29.0 %shard_map.95 = bf16[8,96,768]{2,1,0:T(8,128)(2,1)} custom-call(bf16[8,96,768]{2,1,0:T(8,128)(2,1)} %copy-done.2), custom_call_target="tpu_custom_call" | custom-call | tf_op jit(solution)/shard_map/pallas_call | solution.py:81
  142.0 0.0 copy-start.12
  142.0 1.5 convert_reduce_fusion.1
  143.5 0.1 copy.14
  143.6 0.2 copy.15
  143.8 0.0 copy-done.12
  143.8 0.1 fusion.3
  143.8 0.7 pad_maximum_fusion.3.rows_ref
  144.6 22.2 %shard_map.96 = (bf16[2,8,96,640]{3,2,1,0:T(8,128)(2,1)}, bf16[2,8,40,640]{3,2,1,0:T(8,128)(2,1)}) custom-call(bf16[2,96,640]{2,1,0:T(8,128)(2,1)} %pad_maximum_fusion.3.rows_ref, bf16[2,40,640]{2,1,0:T(8,128)(2,1)} %get-tuple-element.22.wo), custom_call_target="tpu_custom_call" | custom-call | tf_op jit(solution)/shard_map/pallas_call | solution.py:81
  166.8 0.0 copy-start.5
  166.8 1.5 copy-done.5
  168.4 0.0 copy-start.8
  168.4 1.1 copy-done.8
  169.5 1.3 shard_map.97
  170.8 0.0 copy-start.3
  170.8 1.0 copy-done.3
  171.8 22.9 %shard_map.98 = bf16[2,32,24,320]{3,2,1,0:T(8,128)(2,1)} custom-call(bf16[2,32,24,320]{3,2,1,0:T(8,128)(2,1)} %bitcast.43), custom_call_target="tpu_custom_call" | custom-call | tf_op jit(solution)/shard_map/pallas_call | solution.py:81
  194.7 1.5 convert_reduce_fusion
  196.2 0.6 reshape.86
  196.8 0.1 fusion.5
  197.0 0.6 copy.16
  197.6 1.1 squeeze.8
  198.7 0.6 copy.17
  199.4 1.1 squeeze.9
  200.5 1.6 add_convert_fusion
  (11 shorter events, 0.2 us)
Async XLA Ops:
  2.7 2.3 %copy-start.10 = (s32[96,3,640]{2,0,1:T(8,128)S(1)}, s32[96,3,640]{2,0,1:T(8,128)}, u32[]{:S(2)}) copy-start(s32[96,3,640]{2,0,1:T(8,128)} %param.12) | copy-start | bytes 2211844
  5.0 1.0 copy-start.13
  5.0 1.0 copy-start.14
  56.6 3.2 %copy-start = (bf16[2,32,24,2560]{3,2,1,0:T(8,128)(2,1)S(1)}, bf16[2,32,24,2560]{3,2,1,0:T(8,128)(2,1)}, u32[]{:S(2)}) copy-start(bf16[2,32,24,2560]{3,2,1,0:T(8,128)(2,1)} %get-tuple-element.15) | copy-start | bytes 23592964
  59.9 1.7 copy-start.4
  61.6 1.0 copy-start.9
  62.6 5.0 %copy-start.11 = (s32[96,640]{1,0:T(8,128)S(1)}, s32[96,640]{1,0:T(8,128)}, u32[]{:S(2)}) copy-start(s32[96,640]{1,0:T(8,128)} %param.16) | copy-start | bytes 737284
  66.9 0.7 copy-start.6
  103.4 1.5 copy-start.1
  104.9 1.2 copy-start.7
  111.9 1.0 copy-start.2
  142.0 1.8 copy-start.12
  166.8 1.5 copy-start.5
  168.4 1.1 copy-start.8
  170.8 1.0 copy-start.3

commit v3 on v2

--- a/solution.py
+++ b/solution.py
@@ -12,6 +12,7 @@
 NX, NY, NZ, NC = 4, 4, 8, 2
 GROUP = 8
 EPSILON = 1e-06
+VMEM_LIMIT = 60 << 20
 MESH = pl.DeviceIdType.MESH
 BF16 = jnp.bfloat16
 F32 = jnp.float32
@@ -35,14 +36,14 @@
 
 
 class Mover:
-    def __init__(self, send, recv, me):
-        self.send, self.recv, self.me, self.sent = send, recv, me, []
+    def __init__(self, send, recv, me, first=0):
+        self.send, self.recv, self.me, self.first, self.sent = send, recv, me, first, []
 
     def put(self, src, dst, slot, where):
         copy = pltpu.make_async_remote_copy(
             src_ref=src,
             dst_ref=dst,
-            send_sem=self.send.at[len(self.sent)],
+            send_sem=self.send.at[self.first + len(self.sent)],
             recv_sem=self.recv.at[slot],
             device_id=where,
             device_id_type=MESH,
@@ -77,18 +78,21 @@
     return device(there // 2, y, z, there % 2), there
 
 
-def comm(kernel, args, outs, sends, recvs, locals_, collective_id):
+def comm(kernel, args, outs, sends, recvs, locals_, collective_id, scratch=()):
     return pl.pallas_call(
         kernel,
         out_shape=outs,
         in_specs=[pl.BlockSpec(memory_space=pl.ANY)] * len(args),
         out_specs=[pl.BlockSpec(memory_space=pl.ANY)] * len(outs),
-        scratch_shapes=[
+        scratch_shapes=list(scratch)
+        + [
             pltpu.SemaphoreType.DMA((sends,)),
             pltpu.SemaphoreType.DMA((recvs,)),
             pltpu.SemaphoreType.DMA((locals_,)),
         ],
-        compiler_params=pltpu.CompilerParams(collective_id=collective_id, has_side_effects=True),
+        compiler_params=pltpu.CompilerParams(
+            collective_id=collective_id, has_side_effects=True, vmem_limit_bytes=VMEM_LIMIT
+        ),
     )(*args)
 
 
@@ -290,19 +294,25 @@
         y_ref[e] = jnp.where(keep_ref[e : e + 1, :] > 0, unit, normed).astype(BF16)
 
 
-def exchange_kernel(heads, y_ref, mix, wo, kv, q, mixed, wos, send, recv, loc):
+def attention_kernel(
+    heads, factor, y_ref, mix, wo, att, mixg, wog,
+    kv, q, wos, acc, up_out, down_out, up_in, down_in, att_own, send, recv, loc,
+):
     x, y, z, c = place()
     low, high = y % 2, y // 2
     me = device(x, y, z, c)
     own = x * 2 + c
     rows = q.shape[2]
     units = 3 * heads
+    half = att_own.shape[1] // HEAD + 1
+    half = half // 2 * HEAD
     peers = [group_peer(x, y, z, c, d) for d in range(1, GROUP)]
     aligned = [device((x + d) % NX, y, z, c) for d in range(1, NX)]
     twin = device(x, y, z, 1 - c)
     swap = device(x, high * 2 + c, z, low)
     z_up, z_down = device(x, y, (z + 1) % NZ, c), device(x, y, (z + 7) % NZ, c)
     moves = low != c
+    stays = low == c
 
     barrier = pltpu.get_barrier_semaphore()
     for near in [peer for peer, _ in peers] + [z_up, z_down]:
@@ -313,9 +323,13 @@
         pl.semaphore_signal(barrier, inc=1, device_id=swap, device_id_type=MESH)
         pl.semaphore_wait(barrier, GROUP + 2)
 
-    @pl.when(jnp.logical_not(moves))
+    @pl.when(stays)
     def _():
         pl.semaphore_wait(barrier, GROUP + 1)
+
+    Q, R_SWAP, SIGNS, ATT, WO, SUMS = units, units + 14, units + 16, units + 23, units + 30, units + 38
+    FORWARD, SWAP = 14, 14 + 2 * heads
+    mover = Mover(send, recv, me, SWAP + 2)
 
     def copy_to(src, dst, s, r, where):
         return pltpu.make_async_remote_copy(
@@ -326,10 +340,6 @@
             device_id=where,
             device_id_type=MESH,
         )
-
-    RING, FORWARD = 14, 22
-    SWAP = FORWARD + 2 * heads
-    Z, R_SWAP = units, units + 8
 
     def own_copies(n):
         e = n % 2
@@ -358,21 +368,22 @@
                 copy.start()
             kept(n).start()
 
-    swaps = [copy_to(mix, mixed, SWAP, R_SWAP, swap), copy_to(wo, wos, SWAP + 1, R_SWAP + 1, swap)]
-    stays = [
-        pltpu.make_async_copy(mix, mixed, loc.at[2]),
-        pltpu.make_async_copy(wo, wos, loc.at[3]),
-    ]
+    def swapped(part, remote):
+        source = mix if part == 0 else wo
+        landed = mixg.at[x * 2 + low] if part == 0 else wos
+        if remote:
+            return copy_to(source, landed, SWAP + part, R_SWAP + part, swap)
+        return pltpu.make_async_copy(source, landed, loc.at[2 + part])
 
     @pl.when(moves)
     def _():
-        for copy in swaps:
-            copy.start()
-
-    @pl.when(jnp.logical_not(moves))
-    def _():
-        for copy in stays:
-            copy.start()
+        for part in range(2):
+            swapped(part, True).start()
+
+    @pl.when(stays)
+    def _():
+        for part in range(2):
+            swapped(part, False).start()
 
     def arrive(n):
         landed = q.at[z, n] if n < heads else kv.at[n - heads]
@@ -396,40 +407,179 @@
         arrive(n)
 
     cut = (heads + 1) // 2
-    lower, upper = pl.ds(0, cut), pl.ds(cut, heads - cut)
-    ring = []
+    pieces = [pl.ds(0, cut), pl.ds(cut, heads - cut)]
+
+    def q_slot(t, way, piece):
+        return Q + (4 * (t - 1) + 2 * way + piece if t < 4 else 12 + way)
 
     def ring_step(t):
-        down, up = (z + 8 - (t - 1)) % NZ, (z + t - 1) % NZ
-        if t > 1:
-            copy_to(q.at[down], q.at[down], 0, Z + 2 * (t - 2), me).wait_recv()
-            copy_to(q.at[up], q.at[up], 0, Z + 2 * (t - 2) + 1, me).wait_recv()
-        r, s = Z + 2 * (t - 1), RING + 2 * (t - 1)
-        if t < 4:
-            ring.append(copy_to(q.at[down], q.at[down], s, r, z_up))
-            ring.append(copy_to(q.at[up], q.at[up], s + 1, r + 1, z_down))
-        else:
-            ring.append(copy_to(q.at[down, lower], q.at[down, lower], s, r, z_up))
-            ring.append(copy_to(q.at[up, upper], q.at[up, upper], s + 1, r + 1, z_down))
-        ring[-2].start()
-        ring[-1].start()
+        for piece in range(2):
+            for way in range(2):
+                plane = (z + 8 - (t - 1)) % NZ if way == 0 else (z + t - 1) % NZ
+                block = q.at[plane, pieces[piece]]
+                if t > 1:
+                    mover.got(block, q_slot(t - 1, way, piece))
+                if t < 4 or piece == way:
+                    mover.put(block, block, q_slot(t, way, piece), z_down if way else z_up)
+
+    def wo_step(t):
+        for way in range(2):
+            plane = (z + 8 - (t - 1)) % NZ if way == 0 else (z + t - 1) % NZ
+            if t == 1:
+                block = wos
+            else:
+                block = wog.at[:, plane]
+                mover.got(block, WO + 2 * (t - 2) + way)
+            where = z_down if way else z_up
+            if t < 4:
+                mover.put(block, wog.at[:, plane], WO + 2 * (t - 1) + way, where)
+            else:
+                mover.put(wog.at[way, plane], wog.at[way, plane], WO + 6 + way, where)
 
     ring_step(1)
+
+    @pl.when(moves)
+    def _():
+        mover.got(wos, R_SWAP + 1)
+        mover.got(mixg.at[own], R_SWAP)
+
+    @pl.when(stays)
+    def _():
+        for part in range(2):
+            swapped(part, False).wait()
+
+    wo_step(1)
+    wo_own = pltpu.make_async_copy(wos, wog.at[:, z], loc.at[2])
+    wo_own.start()
     for t in range(2, 5):
-        ring_step(t)
         for n in range(heads, units):
             if (n - heads) % 3 == t - 2:
-                arrive(n)
+
+                @pl.when(own == n // 2)
+                def _():
+                    kept(n).wait()
 
                 @pl.when(forwards(n))
                 def _():
+                    landed = kv.at[n - heads]
+                    copy_to(landed, landed, 0, n, me).wait_recv()
                     forward(n).start()
 
+        ring_step(t)
+    wo_step(2)
+    for n in range(heads, units):
+
+        @pl.when(c != (n // 2) % 2)
+        def _():
+            landed = kv.at[n - heads]
+            copy_to(landed, landed, 0, n, me).wait_recv()
+
     far = (z + 4) % NZ
-    copy_to(q.at[far, lower], q.at[far, lower], 0, Z + 6, me).wait_recv()
-    copy_to(q.at[far, upper], q.at[far, upper], 0, Z + 7, me).wait_recv()
-    for copy in ring:
-        copy.wait_send()
+    for way in range(2):
+        mover.got(q.at[far, pieces[way]], q_slot(4, way, way))
+
+    def group_send(source, out, slot):
+        for d, peer in enumerate(aligned):
+            mover.put(source, out.at[own], slot + d, peer)
+        mover.put(source, out.at[own], slot + 3, twin)
+
+    def group_pass(out, slot):
+        for d in (0, 2, 1):
+            there = ((x + NX - 1 - d) % NX) * 2 + c
+            mover.got(out.at[there], slot + d)
+            mover.put(out.at[there], out.at[there], slot + 4 + d, twin)
+
+    def group_end(out, slot):
+        for k in range(NX):
+            mover.got(out.at[own], slot + 3 + k)
+
+    group_send(mixg.at[own], mixg, SIGNS)
+
+    lane = lax.broadcasted_iota(jnp.int32, (rows, HEAD), 1)
+    tail = heads * HEAD
+
+    def plane_sums(planes):
+        for p in planes:
+            acc[p, :, tail:] = jnp.zeros((rows, HEAD), F32)
+
+        def one(head, unused):
+            block = [q[p, head] for p in planes]
+            block = block[0] if len(block) == 1 else jnp.concatenate(block, axis=0)
+            scores = lax.dot_general(
+                block, kv[head], (((1,), (1,)), ((), ())), preferred_element_type=F32
+            )
+            weights = jnp.exp2(scores * factor).astype(BF16)
+            values = kv[heads + head]
+            values = jnp.concatenate([values, jnp.ones_like(values)], axis=1)
+            sums = jnp.dot(weights, values, preferred_element_type=F32)
+            columns = pl.ds(pl.multiple_of(head * HEAD, HEAD), HEAD)
+            for k, p in enumerate(planes):
+                piece = sums[k * rows : (k + 1) * rows]
+                acc[p, :, columns] = piece[:, :HEAD]
+                acc[p, :, tail:] = jnp.where(lane == head, piece[:, HEAD:], acc[p, :, tail:])
+            return unused
+
+        lax.fori_loop(0, heads, one, 0)
+
+    sides = [pl.ds(0, half), pl.ds(half, half)]
+
+    def s_slot(t, way, side):
+        return SUMS + (way if t == 0 else 2 + 4 * (t - 1) + 2 * way + side)
+
+    outs, ins = [up_out, down_out], [up_in, down_in]
+    plane_sums([far])
+    for way in range(2):
+        outs[way][0, :, sides[way]] = acc[far, :, sides[way]].astype(BF16)
+        mover.put(
+            outs[way].at[0, :, sides[way]],
+            ins[way].at[0, :, sides[way]],
+            s_slot(0, way, way),
+            z_down if way else z_up,
+        )
+    for t in range(1, 4):
+        goals = [(z + 4 - t) % NZ, (z + 4 + t) % NZ]
+        plane_sums(goals)
+        for side in range(2):
+            for way in range(2):
+                value = acc[goals[way], :, sides[side]]
+                if t > 1 or side == way:
+                    mover.got(ins[way].at[t - 1, :, sides[side]], s_slot(t - 1, way, side))
+                    value = value + ins[way][t - 1, :, sides[side]].astype(F32)
+                outs[way][t, :, sides[side]] = value.astype(BF16)
+                mover.put(
+                    outs[way].at[t, :, sides[side]],
+                    ins[way].at[t, :, sides[side]],
+                    s_slot(t, way, side),
+                    z_down if way else z_up,
+                )
+        if t == 1:
+            group_pass(mixg, SIGNS)
+    plane_sums([z])
+    wo_step(3)
+    for side in (1, 0):
+        for way in range(2):
+            mover.got(ins[way].at[3, :, sides[side]], s_slot(3, way, side))
+    totals = acc[z, :, tail:]
+    for way in range(2):
+        totals = totals + ins[way][3, :, tail:].astype(F32)
+    for h in range(heads):
+        columns = slice(h * HEAD, (h + 1) * HEAD)
+        value = acc[z, :, columns]
+        for way in range(2):
+            value = value + ins[way][3, :, columns].astype(F32)
+        att_own[:, columns] = (value / totals[:, h : h + 1]).astype(BF16)
+    att_kept = pltpu.make_async_copy(att_own, att.at[own], loc.at[3])
+    att_kept.start()
+    group_send(att_own, att, ATT)
+    wo_step(4)
+    group_pass(att, ATT)
+    group_end(mixg, SIGNS)
+    for way in range(2):
+        mover.got(wog.at[way, far], WO + 6 + way)
+    group_end(att, ATT)
+    wo_own.wait()
+    att_kept.wait()
+    mover.finish()
     for n in range(units):
 
         @pl.when(own == n // 2)
@@ -445,107 +595,16 @@
 
     @pl.when(moves)
     def _():
-        for copy in swaps:
-            copy.wait()
-
-    @pl.when(jnp.logical_not(moves))
-    def _():
-        for copy in stays:
-            copy.wait()
-
-
-def attend_kernel(heads, factor, q_ref, k_ref, v_ref, o_ref):
-    head = pl.program_id(0)
-    planes, rows = q_ref.shape[0], q_ref.shape[2]
-    key_block = k_ref[0]
-    values = jnp.concatenate([v_ref[0], jnp.ones_like(v_ref[0])], axis=1)
-    lane = lax.broadcasted_iota(jnp.int32, (rows, HEAD), 1)
-
-    @pl.when(head == 0)
-    def _():
-        o_ref[:, :, heads * HEAD :] = jnp.zeros((planes, rows, HEAD), BF16)
-
-    for p in range(planes):
-        scores = lax.dot_general(
-            q_ref[p, 0], key_block, (((1,), (1,)), ((), ())), preferred_element_type=F32
-        )
-        weights = jnp.exp2(scores * factor).astype(BF16)
-        sums = jnp.dot(weights, values, preferred_element_type=F32)
-        o_ref[p, :, pl.ds(pl.multiple_of(head * HEAD, HEAD), HEAD)] = sums[:, :HEAD].astype(BF16)
-        held = o_ref[p, :, heads * HEAD :].astype(F32)
-        o_ref[p, :, heads * HEAD :] = jnp.where(lane == head, sums[:, HEAD:], held).astype(BF16)
-
-
-def z_scatter_kernel(part, out, send, recv, loc):
-    x, y, z, c = place()
-    peers = [(device(x, y, (z + d) % NZ, c), (z + d) % NZ) for d in range(1, NZ)]
-    greet([peer for peer, _ in peers], len(peers))
-    mover = Mover(send, recv, device(x, y, z, c))
-    local = pltpu.make_async_copy(part.at[z], out.at[z], loc.at[0])
-    local.start()
-    for d, (peer, there) in enumerate(peers, 1):
-        mover.put(part.at[there], out.at[z], d - 1, peer)
-    for d in range(1, NZ):
-        mover.got(out.at[z], d - 1)
-    local.wait()
-    mover.finish()
-
-
-def group_gather_kernel(rows_ref, wo, out, wog, send, recv, loc):
-    x, y, z, c = place()
-    own = x * 2 + c
-    aligned = [device((x + d) % NX, y, z, c) for d in range(1, NX)]
-    twin = device(x, y, z, 1 - c)
-    z_up, z_down = device(x, y, (z + 1) % NZ, c), device(x, y, (z + 7) % NZ, c)
-    near = aligned + [twin, z_up, z_down]
-    greet(near, len(near))
-    mover = Mover(send, recv, device(x, y, z, c))
-    local = [
-        pltpu.make_async_copy(rows_ref, out.at[:, own], loc.at[0]),
-        pltpu.make_async_copy(wo, wog.at[:, z], loc.at[1]),
-    ]
-    for copy in local:
-        copy.start()
-    TWIN, ZO = 3, 7
-    for d, peer in enumerate(aligned):
-        mover.put(rows_ref, out.at[:, own], d, peer)
-    mover.put(rows_ref, out.at[:, own], TWIN, twin)
-    mover.put(wo, wog.at[:, z], ZO, z_up)
-    mover.put(wo, wog.at[:, z], ZO + 1, z_down)
-
-    def o_next(t):
-        down, up = (z + 8 - t) % NZ, (z + t) % NZ
-        mover.got(wog.at[:, down], ZO + 2 * (t - 1))
-        mover.got(wog.at[:, up], ZO + 2 * (t - 1) + 1)
-        if t < 3:
-            mover.put(wog.at[:, down], wog.at[:, down], ZO + 2 * t, z_up)
-            mover.put(wog.at[:, up], wog.at[:, up], ZO + 2 * t + 1, z_down)
-        else:
-            mover.put(wog.at[0, down], wog.at[0, down], ZO + 6, z_up)
-            mover.put(wog.at[1, up], wog.at[1, up], ZO + 7, z_down)
-
-    order = (0, 2, 1)
-    o_next(1)
-    for step, d in enumerate(order):
-        there = ((x + NX - 1 - d) % NX) * 2 + c
-        mover.got(out.at[:, there], d)
-        mover.put(out.at[:, there], out.at[:, there], TWIN + 1 + d, twin)
-        if step < 2:
-            o_next(2 + step)
-    far = (z + 4) % NZ
-    mover.got(wog.at[0, far], ZO + 6)
-    mover.got(wog.at[1, far], ZO + 7)
-    for k in range(NX):
-        mover.got(out.at[:, own], TWIN + k)
-    for copy in local:
-        copy.wait()
-    mover.finish()
-
-
-def out_kernel(a_ref, w_ref, o_ref):
-    for m in range(2):
+        for part in range(2):
+            swapped(part, True).wait_send()
+
+
+def out_kernel(a_ref, s_ref, w_ref, o_ref):
+    plain = a_ref[...]
+    flipped = (plain.astype(F32) * s_ref[...].astype(F32)).astype(BF16)
+    for m, rows in enumerate((plain, flipped)):
         o_ref[m] = lax.dot_general(
-            a_ref[m], w_ref[m], (((1,), (1,)), ((), ())), preferred_element_type=F32
+            rows, w_ref[m], (((1,), (1,)), ((), ())), preferred_element_type=F32
         ).astype(BF16)
 
 
@@ -634,7 +693,7 @@
             pl.BlockSpec((2, HEAD), lambda i: (0, 0)),
         ],
         out_specs=pl.BlockSpec((2, step, HEAD), lambda i: (0, i, 0)),
-        compiler_params=pltpu.CompilerParams(vmem_limit_bytes=40 << 20),
+        compiler_params=pltpu.CompilerParams(vmem_limit_bytes=VMEM_LIMIT),
     )(
         xg.reshape(2, plane_rows, width),
         wg.reshape(2, width, 2 * HEAD),
@@ -644,63 +703,40 @@
     )
 
     mix = signed(mix_bits).astype(BF16)
-    kv, q, mixed, wo = comm(
-        functools.partial(exchange_kernel, heads),
+    packed = (heads + 1) * HEAD
+    att, mixg, wog = comm(
+        functools.partial(attention_kernel, heads, math.log2(math.e) / math.sqrt(HEAD)),
         (units, mix, wo),
         [
-            jax.ShapeDtypeStruct((2 * heads, plane_rows, HEAD), BF16),
-            jax.ShapeDtypeStruct((NZ, heads, rows, HEAD), BF16),
-            jax.ShapeDtypeStruct(mix.shape, BF16),
-            jax.ShapeDtypeStruct(wo.shape, BF16),
+            jax.ShapeDtypeStruct((GROUP, rows, columns), BF16),
+            jax.ShapeDtypeStruct((GROUP, rows, columns), BF16),
+            jax.ShapeDtypeStruct((2, NZ) + wo.shape[1:], BF16),
         ],
-        24 + 2 * heads,
-        3 * heads + 10,
+        66 + 2 * heads,
+        3 * heads + 52,
         4,
         1,
-    )
-
-    packed = (heads + 1) * HEAD
-    part = pl.pallas_call(
-        functools.partial(attend_kernel, heads, math.log2(math.e) / math.sqrt(HEAD)),
-        grid=(heads,),
-        out_shape=jax.ShapeDtypeStruct((NZ, rows, packed), BF16),
-        in_specs=[
-            pl.BlockSpec((NZ, 1, rows, HEAD), lambda i: (0, i, 0, 0)),
-            pl.BlockSpec((1, plane_rows, HEAD), lambda i: (i, 0, 0)),
-            pl.BlockSpec((1, plane_rows, HEAD), lambda i: (i + heads, 0, 0)),
-        ],
-        out_specs=pl.BlockSpec((NZ, rows, packed), lambda i: (0, 0, 0)),
-        compiler_params=pltpu.CompilerParams(vmem_limit_bytes=40 << 20),
-    )(q, kv, kv)
-
-    (parts,) = comm(z_scatter_kernel, (part,), [jax.ShapeDtypeStruct(part.shape, BF16)], 7, 7, 1, 2)
-    sums = jnp.sum(parts.astype(F32), axis=0)
-    numerator = sums[:, : heads * HEAD].reshape(rows, heads, HEAD)
-    denominator = sums[:, heads * HEAD : heads * HEAD + heads]
-    attended = (numerator / denominator[:, :, None]).astype(BF16).reshape(rows, heads * HEAD)
-    attended_flipped = (attended.astype(F32) * mixed.astype(F32)).astype(BF16)
-    pair = jnp.stack([attended, attended_flipped])
-
-    pairs, wog = comm(
-        group_gather_kernel,
-        (pair, wo),
         [
-            jax.ShapeDtypeStruct((2, GROUP) + pair.shape[1:], BF16),
-            jax.ShapeDtypeStruct((2, NZ) + wo.shape[1:], BF16),
-        ],
-        15,
-        15,
-        2,
-        3,
+            pltpu.VMEM((2 * heads, plane_rows, HEAD), BF16),
+            pltpu.VMEM((NZ, heads, rows, HEAD), BF16),
+            pltpu.VMEM(wo.shape, BF16),
+            pltpu.VMEM((NZ, rows, packed), F32),
+        ]
+        + [pltpu.VMEM((4, rows, packed), BF16)] * 4
+        + [pltpu.VMEM((rows, columns), BF16)],
     )
     out_columns = NZ * wo.shape[1]
     partial_out = pl.pallas_call(
         out_kernel,
         out_shape=jax.ShapeDtypeStruct((2, plane_rows, out_columns), BF16),
-        in_specs=vmem(2),
+        in_specs=vmem(3),
         out_specs=pl.BlockSpec(memory_space=pltpu.VMEM),
-        compiler_params=pltpu.CompilerParams(vmem_limit_bytes=40 << 20),
-    )(pairs.reshape(2, plane_rows, columns), wog.reshape(2, out_columns, columns))
+        compiler_params=pltpu.CompilerParams(vmem_limit_bytes=VMEM_LIMIT),
+    )(
+        att.reshape(plane_rows, columns),
+        mixg.reshape(plane_rows, columns),
+        wog.reshape(2, out_columns, columns),
+    )
 
     count = NX * NY * NC
     (landed,) = comm(

time: 206 us -> 167 us (0.81)
  Pallas kernels: 170 us -> 147 us
  local copies, waits for them, and re-layouts: 22.5 us -> 9.23 us
  other arithmetic: 9.58 us -> 7.29 us
    pallas_call x5 -> x3, Pallas kernels: 158 us -> 135 us  [comm(): pl.pallas_call(kernel, out_shape=outs, in_specs=[pl.BlockSpec(memory_spac...]
    unnamed x30 -> x8, local copies, waits for them, and re-layouts: 14.2 us -> 0.01 us
    pallas_call x1 -> x0, Pallas kernels: 5.82 us -> none  [body(): pl.pallas_call(functools.partial(attend_kernel, heads, math.log2(math.e)...]
    pallas_call x1, Pallas kernels: 4.26 us -> 8.24 us  [body(): pl.pallas_call(project_kernel, grid=(plane_rows // step,), out_shape=jax....]
    pallas_call x1, Pallas kernels: 1.28 us -> 4.04 us  [body(): pl.pallas_call(out_kernel, out_shape=jax.ShapeDtypeStruct((2, plane_rows,...]
where the time goes in v3:
time: 167 us; the launch traced here: 164 us
  Pallas kernels  147 us (88%)
  local copies, waits for them, and re-layouts  9.23 us (6%)
  other arithmetic  7.29 us (4%)
    pallas_call x3, Pallas kernels, comm(): pl.pallas_call(kernel, out_shape=outs, in_specs=[pl.BlockSpec(memory_spac...  135 us
    pallas_call x1, Pallas kernels, body(): pl.pallas_call(project_kernel, grid=(plane_rows // step,), out_shape=jax....  8.24 us
    pallas_call x1, Pallas kernels, body(): pl.pallas_call(out_kernel, out_shape=jax.ShapeDtypeStruct((2, plane_rows,...  4.04 us

profile of v3, /device:TPU:1, one launch (start us, length us, event | category | flops | bytes accessed | tf_op | source)
XLA Modules:
  0.0 164.2 jit_solution(11633149698274486798)
XLA Ops:
  0.0 1.1 fusion.1
  1.1 1.6 pad_maximum_fusion.2.xs
  2.7 0.0 copy-start
  2.7 1.4 reshape.63
  4.2 0.8 copy.22
  5.0 0.0 copy-done
  5.0 0.0 copy-start.2
  5.0 0.0 copy-start.3
  5.0 0.1 fusion
  5.2 0.8 copy.21
  6.0 0.0 copy-done.2
  6.0 0.0 copy-done.3
  6.0 0.6 pad_maximum_fusion.3.gains
  6.6 49.2 %shard_map.91 = (bf16[2,32,24,2560]{3,2,1,0:T(8,128)(2,1)}, bf16[2,4,8,2,40,256]{5,4,3,2,1,0:T(8,128)(2,1)}, bf16[8,96,256]{2,1,0:T(8,128)(2,1)}, f32[2,2,5,128]{3,2,1,0:T(8,128)}) custom-call(bf16[2,24,2560]{2,1,0:T(8,128)(2,1)} %pad_maximum_fusion.2.xs, bf16[8,2,40,256]{3,2,1,0:T(8,128)(2,1)} %bitcast.52, bf16[8,96,256]{2,1,0:T(8,128)(2,1)} %bitcast.48, ...), custom_call_target="tpu_custom_call" | custom-call | tf_op jit(solution)/shard_map/pallas_call | solution.py:82
  55.8 0.7 constant_dynamic-slice_fusion
  56.5 0.6 pad_dynamic-slice_fusion.gain_ref
  57.1 0.7 mul.49.keep_ref
  57.8 0.0 copy-start.1
  57.8 8.2 %shard_map.92.y_ref = bf16[2,768,128]{2,1,0:T(8,128)(2,1)} custom-call(bf16[2,768,2560]{2,1,0:T(8,128)(2,1)} %bitcast.39, bf16[2,2560,256]{2,1,0:T(8,128)(2,1)} %bitcast.43, bf16[768,256]{1,0:T(8,128)(2,1)} %bitcast.57, f32[2,128]{1,0:T(2,128)} %pad_dynamic-slice_fusion.gain_ref, f32[2,128]{1,0:T(2,128)} %mul.49.keep_ref), custom_call_target="tpu_custom_call" | custom-call | tf_op jit(solution)/shard_map/pallas_call | solution.py:684
  66.0 0.0 copy-done.1
  66.0 0.7 convert_convert_fusion.1.mix
  66.7 65.7 %shard_map.93 = (bf16[8,96,640]{2,1,0:T(8,128)(2,1)}, bf16[8,96,640]{2,1,0:T(8,128)(2,1)}, bf16[2,8,40,640]{3,2,1,0:T(8,128)(2,1)}) custom-call(bf16[2,768,128]{2,1,0:T(8,128)(2,1)} %shard_map.92.y_ref, bf16[96,640]{1,0:T(8,128)(2,1)} %convert_convert_fusion.1.mix, bf16[2,40,640]{2,1,0:T(8,128)(2,1)} %bitcast.58), custom_call_target="tpu_custom_call" | custom-call | tf_op jit(solution)/shard_map/pallas_call | solution.py:82
  132.4 4.0 %shard_map.94 = bf16[2,768,320]{2,1,0:T(8,128)(2,1)} custom-call(bf16[768,640]{1,0:T(8,128)(2,1)} %bitcast.53, bf16[768,640]{1,0:T(8,128)(2,1)} %bitcast.54, bf16[2,320,640]{2,1,0:T(8,128)(2,1)} %bitcast.55), custom_call_target="tpu_custom_call" | custom-call | tf_op jit(solution)/shard_map/pallas_call | solution.py:729
  136.5 20.3 %shard_map.95 = bf16[2,32,24,320]{3,2,1,0:T(8,128)(2,1)} custom-call(bf16[2,32,24,320]{3,2,1,0:T(8,128)(2,1)} %bitcast.42), custom_call_target="tpu_custom_call" | custom-call | tf_op jit(solution)/shard_map/pallas_call | solution.py:82
  156.8 1.5 convert_reduce_fusion
  158.3 0.6 reshape.79
  158.9 0.1 fusion.2
  159.0 0.6 copy.14
  159.6 1.1 squeeze.8
  160.8 0.6 copy.15
  161.4 1.1 squeeze.9
  162.6 1.6 %add_convert_fusion = bf16[24,2560]{1,0:T(8,128)(2,1)} fusion(f32[24,2560]{1,0:T(8,128)S(1)} %squeeze.8, f32[24,2560]{1,0:T(8,128)S(1)} %squeeze.9, s32[96,2560]{1,0:T(8,128)} %param.17, s32[]{:T(128)S(6)} %select_n.39), kind=kLoop, calls=%fused_computation.8 | loop fusion | flops 368640 | bytes 860164 | tf_op jit(solution)/shard_map/convert_element_type | solution.py:755
  (8 shorter events, 0.2 us)
Async XLA Ops:
  2.7 2.3 %copy-start = (s32[96,3,640]{2,0,1:T(8,128)S(1)}, s32[96,3,640]{2,0,1:T(8,128)}, u32[]{:S(2)}) copy-start(s32[96,3,640]{2,0,1:T(8,128)} %param.12) | copy-start | bytes 2211844
  5.0 1.0 copy-start.2
  5.0 1.0 copy-start.3
  57.8 8.2 %copy-start.1 = (s32[96,640]{1,0:T(8,128)S(1)}, s32[96,640]{1,0:T(8,128)}, u32[]{:S(2)}) copy-start(s32[96,640]{1,0:T(8,128)} %param.16) | copy-start | bytes 737284
